TPU v7x, 32 devices: a whole 2x2x4 slice. The times are simulated.
32 devices in a mesh: chan: 8 (over y, x, core), facet: 4 (over z).
Axes of the slice: x: 2, y: 2, z: 4, core: 2. Of those that a mesh axis runs over, the one named last changes fastest.
Arguments:
- x_init: float32 [128, 256, 2048], P('chan', 'facet'), may hold values from 0 to 2
- u_init: float32 [128, 2, 256, 2048], P('chan', None, 'facet')
- v_init: float32 [128, 32, 2, 128], P('chan'), may hold values from -4 to 4
- observed: float32 [128, 32, 2, 128], P('chan'), may hold values from -6 to 6
- tiles: bfloat16 [128, 32, 2, 128, 128], P('chan'), may hold values from -0.375 to 0.375
- pattern: int32 [128, 32, 2], P('chan'), may hold values from 0 to 4095
- counts: int32 [128], P('chan'), may hold values from 1 to 32, as said below
- facet_bounds: int32 [4, 2], replicated, may hold values from 0 to 256, as said below
Outputs:
- image: float32 [128, 256, 2048], P('chan', 'facet')
- prior_dual: float32 [128, 2, 256, 2048], P('chan', None, 'facet')
- data_dual: float32 [128, 32, 2, 128], P('chan')
Inputs may be any that keep to these rules, and one draw needn't show every extreme that they name: `counts`: channels 128 - 128/4 to 127 hold 32 live blocks each; the others hold fewer than half of 32, and at least one. `facet_bounds`: facet 0 starts at row 0 and the last facet ends at row 256; facets are in order, and each facet after the first starts one to 16 rows before the previous one ends, so every row lies in one or two facets.
All inputs are finite; a program needn't handle non-finite values.
Results may differ from a plain program's by a relative error of at most 0.0032.
Values sent between devices are 32-bit elements; how exact they have to be, the bound alone decides.
No kernel may reach another device: no remote copies, remote signals or barrier semaphores. Data moves between devices by JAX's collectives and lax.ppermute only.
A program may use at most 256 MiB of HBM per device.

v0:
```python
import math

import jax
import jax.numpy as jnp
from jax import lax
from jax.sharding import PartitionSpec as P

ITERS = 2


STEP_PRIMAL = 0.5
STEP_PRIOR = 0.5
STEP_DATA = 1.0
RADIUS = 12.0
ROOT_HALF = 0.7071067811865476


def shifted(shard, axis, by):
    count = lax.axis_size(axis)
    pairs = [(i, i + by) for i in range(count) if 0 <= i + by < count]
    return lax.ppermute(shard, axis, pairs)


def dft_table(extent, tile_side):
    column = jnp.arange(2 * extent, dtype=jnp.int32)
    is_sine = column // tile_side % 2
    frequency = column // (2 * tile_side) * tile_side + column % tile_side
    row_index = jnp.arange(extent, dtype=jnp.int32)
    phases = row_index[:, None] * frequency[None, :] % extent
    angles = phases.astype(jnp.float32) * (2.0 * math.pi / extent)
    values = jnp.where(is_sine[None, :] == 0, jnp.cos(angles), -jnp.sin(angles))
    return (values / math.sqrt(extent)).astype(jnp.bfloat16)


def analysis(image):
    arrived = shifted(image[:, :1, :], "facet", -1)
    below = jnp.concatenate([image[:, 1:], arrived], axis=1)
    right = jnp.concatenate([image[:, :, 1:], jnp.zeros_like(image[:, :, :1])], axis=2)
    return jnp.stack([below - image, right - image], axis=1) * ROOT_HALF


def synthesis(coeffs):
    vertical = coeffs[:, 0]
    horizontal = coeffs[:, 1]
    carried = shifted(vertical[:, -1:, :], "facet", 1)
    above = jnp.concatenate([carried, vertical[:, :-1]], axis=1)
    leftward = jnp.concatenate(
        [jnp.zeros_like(horizontal[:, :, :1]), horizontal[:, :, :-1]], axis=2
    )
    return (above - vertical + leftward - horizontal) * ROOT_HALF


def measure_all(grid, tiles, safe_index, keep):
    picked = jax.vmap(lambda grid_one, index_one: grid_one[index_one])(grid, safe_index)
    picked = jnp.where(keep[..., None, None], picked, jnp.zeros_like(picked))
    return jnp.einsum("cbkrg,cbkvg->cbrv", picked, tiles, preferred_element_type=jnp.float32)


def spread_all(weights, tiles, flat_index, keep, blocks_total):
    tile_side = tiles.shape[-1]
    contrib = jnp.einsum("cbrv,cbkvg->cbkrg", weights, tiles, preferred_element_type=jnp.float32)
    contrib = jnp.where(keep[..., None, None], contrib, 0.0)
    empty = jnp.zeros((blocks_total, 2, tile_side), jnp.float32)
    return empty.at[flat_index.reshape(-1)].add(contrib.reshape(-1, 2, tile_side))


def local(x_init, u_init, v_init, observed, tiles, pattern, counts, facet_bounds):
    chans, rows_here, extent = x_init.shape
    slot_count = tiles.shape[1]
    tile_side = tiles.shape[-1]
    per_row = extent // tile_side
    blocks_here = rows_here * per_row
    row_start = lax.axis_index("facet") * rows_here
    table = dft_table(extent, tile_side)
    live = jnp.arange(slot_count, dtype=jnp.int32)[None, :] < counts[:, None]
    live_float = live.astype(jnp.float32)
    local_index = pattern - row_start * per_row
    owned = (local_index >= 0) & (local_index < blocks_here)
    keep = owned & live[:, :, None]
    safe_index = jnp.clip(local_index, 0, blocks_here - 1)
    flat_index = safe_index + (jnp.arange(chans, dtype=jnp.int32) * blocks_here)[:, None, None]
    row_ids = row_start + jnp.arange(rows_here, dtype=jnp.int32)
    inside = (row_ids[None, :] >= facet_bounds[:, 0:1]) & (row_ids[None, :] < facet_bounds[:, 1:2])
    cover = jnp.sum(inside.astype(jnp.float32), axis=0)
    radius = RADIUS / cover
    image, prior_dual, data_dual = (x_init, u_init, v_init)
    for rounds in range(ITERS):
        weights = data_dual.astype(jnp.bfloat16)
        grid_adj = spread_all(weights, tiles, flat_index, keep, chans * blocks_here)
        grid_adj = grid_adj.reshape(chans * rows_here, 2 * extent).astype(jnp.bfloat16)
        back = lax.dot_general(
            grid_adj, table, (((1,), (1,)), ((), ())), preferred_element_type=jnp.float32
        )
        back = back.reshape(chans, rows_here, extent)
        image_next = jnp.maximum(image - STEP_PRIMAL * (synthesis(prior_dual) + back), 0.0)
        extrap = 2.0 * image_next - image
        pushed = prior_dual + STEP_PRIOR * analysis(extrap)
        local_sum = jnp.sum(pushed * pushed, axis=0)
        total = lax.psum(local_sum, "chan")
        norms = jnp.sqrt(total + 1e-06)
        prior_dual = pushed * jnp.minimum(1.0, radius[None, None, :, None] / norms[None])
        grid = jnp.dot(
            extrap.reshape(chans * rows_here, extent).astype(jnp.bfloat16),
            table,
            preferred_element_type=jnp.float32,
        )
        grid = grid.astype(jnp.bfloat16).reshape(chans, blocks_here, 2, tile_side)
        partial_vis = measure_all(grid, tiles, safe_index, keep)
        seen = lax.psum(partial_vis, "facet")
        data_dual = (
            (data_dual + STEP_DATA * (seen - observed))
            * live_float[:, :, None, None]
            / (1.0 + STEP_DATA)
        )
        image = image_next
    return (image, prior_dual, data_dual)


def solution(mesh):
    in_specs = (
        P("chan", "facet", None),
        P("chan", None, "facet", None),
        P("chan", None, None, None),
        P("chan", None, None, None),
        P("chan", None, None, None, None),
        P("chan", None, None),
        P("chan"),
        P(),
    )
    out_specs = (
        P("chan", "facet", None),
        P("chan", None, "facet", None),
        P("chan", None, None, None),
    )
    return jax.shard_map(local, mesh=mesh, in_specs=in_specs, out_specs=out_specs, check_vma=False)
```

profile of v0, /device:TPU:0, one launch (start us, length us, event | category | flops | bytes accessed | tf_op | source)
XLA Modules:
  0.0 1365.7 jit_solution(8844238610441799754)
XLA Ops:
  7.2 10.0 slice_bitcast_fusion.2
  22.3 136.9 %fusion.33.clone.4 = bf16[2048,4096,1]{1,0,2:T(8,128)(2,1)} fusion(s32[4096]{0:T(1024)S(1)} %fusion.52, pred[4096]{0:T(1024)(128)(4,1)S(1)} %fusion.49), kind=kLoop, calls=%fused_computation.21.clone.clone.clone.clone.clone.1 | loop fusion | flops 150994944 | bytes 16797696 | tf_op jit(solution)/shard_map/convert_element_type | solution.py:103
  159.2 136.9 %multiply_convert_fusion.11 = bf16[2048,4096]{1,0:T(8,128)(2,1)} fusion(s32[4096]{0:T(1024)S(1)} %fusion.52, pred[4096]{0:T(1024)(128)(4,1)S(1)} %fusion.49), kind=kLoop, calls=%fused_computation.10.clone.2.clone.clone.clone.1 | loop fusion | flops 150994944 | bytes 16797696 | tf_op jit(solution)/shard_map/dot_general | solution.py:102
  296.1 137.4 %fusion.35.clone.4 = bf16[2048,4096,1]{1,0,2:T(8,128)(2,1)} fusion(s32[4096]{0:T(1024)S(1)} %fusion.52, pred[4096]{0:T(1024)(128)(4,1)S(1)} %fusion.49), kind=kLoop, calls=%fused_computation.19.clone.clone.clone.clone.clone.1 | loop fusion | flops 150994944 | bytes 16797696 | tf_op jit(solution)/shard_map/convert_element_type | solution.py:103
  433.5 137.0 %multiply_convert_fusion.12 = bf16[2048,4096]{1,0:T(8,128)(2,1)} fusion(s32[4096]{0:T(1024)S(1)} %fusion.52, pred[4096]{0:T(1024)(128)(4,1)S(1)} %fusion.49), kind=kLoop, calls=%fused_computation.10.clone.1.clone.clone.clone | loop fusion | flops 150994944 | bytes 16797696 | tf_op jit(solution)/shard_map/dot_general | solution.py:102
  571.9 12.4 convolution_select_fusion.1
  590.5 121.7 %scatter_fusion = f32[16384,2,128]{2,1,0:T(2,128)} fusion(f32[16384,2,128]{2,1,0:T(2,128)} %broadcast.239.clone, s32[1024]{0:T(1024)S(1)} %bitcast.109, f32[1024,2,128]{2,1,0:T(2,128)S(1)} %bitcast.105), kind=kCustom, calls=%fused_computation.2 | custom fusion | flops 262144 | bytes 3149824 | tf_op jit(solution)/shard_map/scatter-add | solution.py:64
  712.1 9.5 convert_element_type.67
  721.7 14.4 %convert_element_type.68 = bf16[16,64,4096]{2,1,0:T(8,128)(2,1)} reshape(bf16[16384,2,128]{2,1,0:T(2,128)(2,1)} %convert_element_type.67) | data formatting | bytes 16777216 | tf_op jit(solution)/shard_map/convert_element_type | solution.py:90
  736.6 34.5 %fusion.83 = (bf16[16,64,2048]{2,1,0:T(8,128)(2,1)}, f32[16,64,2048]{2,1,0:T(8,128)}, f32[16,64,2048]{2,1,0:T(8,128)}) fusion(f32[16,64,2048]{2,1,0:T(8,128)} %param.8, bf16[16,64,4096]{2,1,0:T(8,128)(2,1)} %convert_element_type.68, f32[16,64,2047]{2,1,0:T(8,128)} %bitcast.103, f32[16,63,2048]{2,1,0:T(8,128)} %bitcast.101, ...), kind=kOutput, calls=%fused_computation.136 | convolution fusion | flops 17205035008 | bytes 88076288 | tf_op jit(solution)/shard_map/dot_general | solution.py:91
  773.7 22.9 %fusion.30 = bf16[1024,4096]{1,0:T(8,128)(2,1)} fusion(bf16[1024,2048]{1,0:T(8,128)(2,1)} %bitcast.111, bf16[2048,4096]{1,0:T(8,128)(2,1)} %multiply_convert_fusion.11), kind=kOutput, calls=%fused_computation.56 | convolution fusion | flops 17184063488 | bytes 29360128 | tf_op jit(solution)/shard_map/dot_general | solution.py:102
  806.5 14.2 %reshape.173 = bf16[16,1024,2,128]{3,2,1,0:T(2,128)(2,1)} reshape(bf16[1024,4096]{1,0:T(8,128)(2,1)} %fusion.30) | data formatting | bytes 16777216 | tf_op jit(solution)/shard_map/reshape | solution.py:107
  828.5 13.7 %fusion.21 = (f32[16,1,64,2048]{3,2,0,1:T(8,128)S(1)}, f32[16,1,64,2048]{3,2,0,1:T(8,128)}) fusion(f32[16,64,2048]{2,1,0:T(8,128)} %get-tuple-element.15, f32[16,1,2048]{2,1,0:T(1,128)S(1)} %collective-permute-done.1, f32[16,63,2048]{2,1,0:T(8,128)} %slice.81, f32[16,64,2047]{2,1,0:T(8,128)} %slice.83), kind=kLoop, calls=%fused_computation.39 | loop fusion | flops 6291456 | bytes 41938944 | tf_op jit(solution)/shard_map/stack | solution.py:39
  845.4 10.7 multiply_reduce_fusion.1
  856.2 15.5 %convolution_bitcast_fusion.1 = f32[16,32,2,128]{3,2,1,0:T(2,128)} fusion(bf16[16,32,2,128,128]{4,3,2,1,0:T(8,128)(2,1)} %param.12, bf16[16,32,2,2,128]{4,3,2,1,0:T(2,128)(2,1)S(1)} %bitcast.107, pred[16,32,2]{2,1,0:T(8,128)(4,1)S(1)} %copy.30), kind=kOutput, calls=%fused_computation.60 | convolution fusion | flops 67371008 | bytes 34604032 | tf_op jit(solution)/shard_map/cbkrg,cbkvg->cbrv/dot_general | solution.py:56
  871.8 41.8 %all-reduce.9.cloned.1.call-done = f32[2,64,2048]{2,1,0:T(8,128)} async-done(((f32[2,64,2048]{2,1,0:T(8,128)}), f32[2,64,2048]{2,1,0:T(8,128)}) %all-reduce.9.cloned.1.call-update) | async-done | bytes 1048592 | tf_op jit(solution)/shard_map/psum | solution.py:99
  916.1 11.9 broadcast_multiply_fusion.1
  943.7 11.3 all-reduce.11.cloned.1.call-done
  955.0 13.5 convolution_select_fusion
  974.6 121.7 %scatter_fusion.1 = f32[16384,2,128]{2,1,0:T(2,128)} fusion(f32[16384,2,128]{2,1,0:T(2,128)} %broadcast.239, s32[1024]{0:T(1024)S(1)} %bitcast.110, f32[1024,2,128]{2,1,0:T(2,128)S(1)} %bitcast.106), kind=kCustom, calls=%fused_computation.3 | custom fusion | flops 262144 | bytes 3149824 | tf_op jit(solution)/shard_map/scatter-add | solution.py:64
  1096.3 9.3 convert_element_type.77
  1105.6 14.4 %convert_element_type.78 = bf16[16,64,4096]{2,1,0:T(8,128)(2,1)} reshape(bf16[16384,2,128]{2,1,0:T(2,128)(2,1)} %convert_element_type.77) | data formatting | bytes 16777216 | tf_op jit(solution)/shard_map/convert_element_type | solution.py:90
  1120.0 34.5 %fusion.82 = (bf16[16,64,2048]{2,1,0:T(8,128)(2,1)}, f32[16,64,2048]{2,1,0:T(8,128)}, f32[16,64,2048]{2,1,0:T(8,128)}) fusion(f32[16,64,2048]{2,1,0:T(8,128)} %get-tuple-element.28, bf16[16,64,4096]{2,1,0:T(8,128)(2,1)} %convert_element_type.78, f32[16,2,64,2048]{3,2,0,1:T(8,128)} %copy-done.5, f32[16,64,2047]{2,1,0:T(8,128)} %bitcast.104, ...), kind=kOutput, calls=%fused_computation.135 | convolution fusion | flops 17205035008 | bytes 88076288 | tf_op jit(solution)/shard_map/dot_general | solution.py:91
  1154.5 22.8 %fusion.31 = bf16[1024,4096]{1,0:T(8,128)(2,1)} fusion(bf16[1024,2048]{1,0:T(8,128)(2,1)} %bitcast.112, bf16[2048,4096]{1,0:T(8,128)(2,1)} %multiply_convert_fusion.12), kind=kOutput, calls=%fused_computation.57 | convolution fusion | flops 17184063488 | bytes 29360128 | tf_op jit(solution)/shard_map/dot_general | solution.py:102
  1177.3 14.3 %reshape.175 = bf16[16,1024,2,128]{3,2,1,0:T(2,128)(2,1)} reshape(bf16[1024,4096]{1,0:T(8,128)(2,1)} %fusion.31) | data formatting | bytes 16777216 | tf_op jit(solution)/shard_map/reshape | solution.py:107
  1202.2 15.4 %convolution_bitcast_fusion = f32[16,32,2,128]{3,2,1,0:T(2,128)} fusion(bf16[16,32,2,128,128]{4,3,2,1,0:T(8,128)(2,1)} %param.12, bf16[16,32,2,2,128]{4,3,2,1,0:T(2,128)(2,1)S(1)} %bitcast.108, pred[16,32,2]{2,1,0:T(8,128)(4,1)S(1)} %copy.30), kind=kOutput, calls=%fused_computation.59 | convolution fusion | flops 67371008 | bytes 34604032 | tf_op jit(solution)/shard_map/cbkrg,cbkvg->cbrv/dot_general | solution.py:56
  1217.6 8.7 slice.89
  1226.3 8.8 slice.91
  1235.2 14.0 %fusion.29 = (f32[16,1,64,2048]{3,2,0,1:T(8,128)S(1)}, f32[16,1,64,2048]{3,2,0,1:T(8,128)}) fusion(f32[16,64,2048]{2,1,0:T(8,128)} %get-tuple-element.13, f32[16,1,2048]{2,1,0:T(1,128)S(1)} %collective-permute-done.3, f32[16,63,2048]{2,1,0:T(8,128)} %slice.89, f32[16,64,2047]{2,1,0:T(8,128)} %slice.91), kind=kLoop, calls=%fused_computation.49 | loop fusion | flops 6291456 | bytes 41938944 | tf_op jit(solution)/shard_map/stack | solution.py:39
  1252.6 16.5 %multiply_reduce_fusion = f32[2,64,2048]{2,1,0:T(8,128)} fusion(f32[16,1,64,2048]{3,2,0,1:T(8,128)} %get-tuple-element.21, f32[16,1,64,2048]{3,2,0,1:T(8,128)S(1)} %get-tuple-element.20, f32[2,64,2048]{2,1,0:T(8,128)S(1)} %copy-done.7, f32[16,1,64,2048]{3,2,0,1:T(8,128)} %get-tuple-element.23, f32[16,1,64,2048]{3,2,0,1:T(8,128)} %copy-done.2, ...), kind=kLoop, calls=%fused_computation.22 | loop fusion | flops 37486592 | bytes 52428800 | tf_op jit(solution)/shard_map/reduce_sum | solution.py:98
  1276.9 57.2 %all-reduce.13.cloned.1.call-done = f32[2,64,2048]{2,1,0:T(8,128)} async-done(((f32[2,64,2048]{2,1,0:T(8,128)}), f32[2,64,2048]{2,1,0:T(8,128)}) %all-reduce.13.cloned.1.call-update) | async-done | bytes 1048592 | tf_op jit(solution)/shard_map/psum | solution.py:99
  1335.5 17.2 %broadcast_multiply_fusion = f32[16,2,64,2048]{3,2,0,1:T(8,128)S(1)} fusion(f32[2,64,2048]{2,1,0:T(8,128)S(1)} %multiply_minimum_fusion, f32[16,1,64,2048]{3,2,0,1:T(8,128)} %get-tuple-element.21, f32[16,1,64,2048]{3,2,0,1:T(8,128)} %copy-done.4, f32[2,64,2048]{2,1,0:T(8,128)S(1)} %copy-done.7, f32[16,1,64,2048]{3,2,0,1:T(8,128)} %get-tuple-element.23, ...), kind=kLoop, calls=%fused_computation.50 | loop fusion | flops 33554432 | bytes 69206016 | tf_op jit(solution)/shard_map/mul | solution.py:101
  (97 shorter events, 90.3 us)
Async XLA Ops:
  7.2 906.5 %all-reduce.9.cloned.1.call-start = ((), (), s32[]{:S(2)}) async-start(), calls=%async_computation | async-start | bytes 2097152 | tf_op jit(solution)/shard_map/psum | solution.py:99
  17.2 278.9 %copy-start.8 = (f32[16,64,2048]{2,1,0:T(8,128)}, f32[16,64,2048]{2,1,0:T(8,128)S(1)}, u32[]{:S(2)}) copy-start(f32[16,64,2048]{2,1,0:T(8,128)S(1)} %get-tuple-element.19) | copy-start | bytes 25165828
  17.3 719.3 %collective-permute-start = (f32[16,1,2048]{2,1,0:T(1,128)S(1)}, f32[16,1,2048]{2,1,0:T(1,128)S(1)}, u32[]{:S(2)}, u32[]{:S(2)}) collective-permute-start(f32[16,1,2048]{2,1,0:T(1,128)S(1)} %slice.77), channel_id=1, source_target_pairs={{0,1},{1,2},{2,3},{4,5},{5,6},{6,7},{8,9},{9,10},{10,11},{12,13},{... | collective-permute-start | bytes 393224 | tf_op jit(solution)/shard_map/ppermute | solution.py:21
  433.5 137.0 %copy-start.23 = (s32[16]{0:T(128)S(1)}, s32[16]{0:T(128)}, u32[]{:S(2)}) copy-start(s32[16]{0:T(128)} %param.14) | copy-start | bytes 196
  433.5 137.6 %copy-start.15 = (s32[16,32,2]{1,2,0:T(2,128)S(1)}, s32[16,32,2]{1,2,0:T(2,128)}, u32[]{:S(2)}) copy-start(s32[16,32,2]{1,2,0:T(2,128)} %param.13) | copy-start | bytes 12292
  433.5 138.4 %copy-start.9 = (f32[16,32,2,128]{3,2,1,0:T(2,128)S(1)}, f32[16,32,2,128]{3,2,1,0:T(2,128)}, u32[]{:S(2)}) copy-start(f32[16,32,2,128]{3,2,1,0:T(2,128)} %param.10) | copy-start | bytes 1572868
  571.9 18.5 %copy-start.16 = (s32[1024,1]{0,1:T(1,128)}, s32[1024,1]{0,1:T(1,128)S(1)}, u32[]{:S(2)}) copy-start(s32[1024,1]{0,1:T(1,128)S(1)} %compare_select_fusion.1) | copy-start | bytes 12292
  712.1 23.9 %copy-start.22 = (s32[4,2]{0,1:T(2,128)S(1)}, s32[4,2]{0,1:T(2,128)}, u32[]{:S(2)}) copy-start(s32[4,2]{0,1:T(2,128)} %param.15) | copy-start | bytes 100
  736.4 84.2 %copy-start = (s32[1024]{0:T(1024)}, s32[1024]{0:T(1024)S(1)}, u32[]{:S(2)}) copy-start(s32[1024]{0:T(1024)S(1)} %reshape.176) | copy-start | bytes 12292
  736.5 177.1 %copy-start.20 = (f32[64]{0:T(128)}, f32[64]{0:T(128)S(1)}, u32[]{:S(2)}) copy-start(f32[64]{0:T(128)S(1)} %broadcast_divide_fusion) | copy-start | bytes 772
  772.4 56.1 %collective-permute-start.1 = (f32[16,1,2048]{2,1,0:T(1,128)S(1)}, f32[16,1,2048]{2,1,0:T(1,128)S(1)}, u32[]{:S(2)}, u32[]{:S(2)}) collective-permute-start(f32[16,1,2048]{2,1,0:T(1,128)S(1)} %slice.82), channel_id=1, source_target_pairs={{1,0},{2,1},{3,2},{5,4},{6,5},{7,6},{9,8},{10,9},{11,10},{13,12},{... | collective-permute-start | bytes 393224 | tf_op jit(solution)/shard_map/ppermute | solution.py:21
  773.7 23.0 %copy-start.3 = (f32[16,64,2048]{2,1,0:T(8,128)S(1)}, f32[16,64,2048]{2,1,0:T(8,128)}, u32[]{:S(2)}) copy-start(f32[16,64,2048]{2,1,0:T(8,128)} %get-tuple-element.15) | copy-start | bytes 25165828
  842.2 3.2 copy-start.2
  856.2 98.8 %all-reduce.11.cloned.1.call-start = ((), (), s32[]{:S(2)}) async-start(), calls=%async_computation.1 | async-start | bytes 1048576 | tf_op jit(solution)/shard_map/psum | solution.py:109
  871.7 402.7 %all-reduce.15.cloned.1.call-start = ((), (), s32[]{:S(2)}) async-start(), calls=%async_computation.3 | async-start | bytes 1048576 | tf_op jit(solution)/shard_map/psum | solution.py:109
  915.1 1.0 copy-start.6
  928.0 11.1 copy-start.5
  928.0 26.9 %copy-start.10 = (f32[16,32,2,128]{3,2,1,0:T(2,128)S(1)}, f32[16,32,2,128]{3,2,1,0:T(2,128)}, u32[]{:S(2)}) copy-start(f32[16,32,2,128]{3,2,1,0:T(2,128)} %param.10) | copy-start | bytes 1572868
  928.0 26.9 %copy-start.12 = (f32[16,32,2,128]{3,2,1,0:T(2,128)S(1)}, f32[16,32,2,128]{3,2,1,0:T(2,128)}, u32[]{:S(2)}) copy-start(f32[16,32,2,128]{3,2,1,0:T(2,128)} %param.11) | copy-start | bytes 1572868
  928.1 26.9 %copy-start.18 = (f32[16,32]{1,0:T(8,128)S(1)}, f32[16,32]{1,0:T(8,128)}, u32[]{:S(2)}) copy-start(f32[16,32]{1,0:T(8,128)} %get-tuple-element.26) | copy-start | bytes 6148
  940.5 179.5 %collective-permute-start.2 = (f32[16,1,2048]{2,1,0:T(1,128)S(1)}, f32[16,1,2048]{2,1,0:T(1,128)S(1)}, u32[]{:S(2)}, u32[]{:S(2)}) collective-permute-start(f32[16,1,2048]{2,1,0:T(1,128)S(1)} %slice.85), channel_id=1, source_target_pairs={{0,1},{1,2},{2,3},{4,5},{5,6},{6,7},{8,9},{9,10},{10,11},{12,13},{... | collective-permute-start | bytes 393224 | tf_op jit(solution)/shard_map/ppermute | solution.py:21
  968.5 6.1 copy-start.17
  1177.3 14.3 %copy-start.1 = (s32[1024]{0:T(1024)S(1)}, s32[1024]{0:T(1024)}, u32[]{:S(2)}) copy-start(s32[1024]{0:T(1024)} %copy-done) | copy-start | bytes 12292
  1200.9 34.3 %collective-permute-start.3 = (f32[16,1,2048]{2,1,0:T(1,128)S(1)}, f32[16,1,2048]{2,1,0:T(1,128)S(1)}, u32[]{:S(2)}, u32[]{:S(2)}) collective-permute-start(f32[16,1,2048]{2,1,0:T(1,128)S(1)} %slice.90), channel_id=1, source_target_pairs={{1,0},{2,1},{3,2},{5,4},{6,5},{7,6},{9,8},{10,9},{11,10},{13,12},{... | collective-permute-start | bytes 393224 | tf_op jit(solution)/shard_map/ppermute | solution.py:21
  1235.1 17.4 %copy-start.7 = (f32[2,64,2048]{2,1,0:T(8,128)S(1)}, f32[2,64,2048]{2,1,0:T(8,128)}, u32[]{:S(2)}) copy-start(f32[2,64,2048]{2,1,0:T(8,128)} %copy-done.6) | copy-start | bytes 3145732
  1235.1 98.9 %all-reduce.13.cloned.1.call-start = ((), (), s32[]{:S(2)}) async-start(), calls=%async_computation.2 | async-start | bytes 2097152 | tf_op jit(solution)/shard_map/psum | solution.py:99
  1249.2 3.4 copy-start.4
  1252.6 21.8 %copy-start.11 = (f32[16,32,2,128]{3,2,1,0:T(2,128)S(1)}, f32[16,32,2,128]{3,2,1,0:T(2,128)}, u32[]{:S(2)}) copy-start(f32[16,32,2,128]{3,2,1,0:T(2,128)} %param.10) | copy-start | bytes 1572868
  1252.6 21.8 %copy-start.13 = (f32[16,32,2,128]{3,2,1,0:T(2,128)S(1)}, f32[16,32,2,128]{3,2,1,0:T(2,128)}, u32[]{:S(2)}) copy-start(f32[16,32,2,128]{3,2,1,0:T(2,128)} %param.11) | copy-start | bytes 1572868
  1252.6 21.8 %copy-start.14 = (f32[16,32,2,128]{3,2,1,0:T(2,128)S(1)}, f32[16,32,2,128]{3,2,1,0:T(2,128)}, u32[]{:S(2)}) copy-start(f32[16,32,2,128]{3,2,1,0:T(2,128)} %all-reduce.11.cloned.1.call-done) | copy-start | bytes 1572868
  1252.6 21.8 %copy-start.19 = (f32[16,32]{1,0:T(8,128)S(1)}, f32[16,32]{1,0:T(8,128)}, u32[]{:S(2)}) copy-start(f32[16,32]{1,0:T(8,128)} %get-tuple-element.26) | copy-start | bytes 6148
  1252.6 81.5 %copy-start.21 = (f32[64]{0:T(128)S(1)}, f32[64]{0:T(128)}, u32[]{:S(2)}) copy-start(f32[64]{0:T(128)} %copy-done.20) | copy-start | bytes 772
Sparse Core Ops, SparseCore 0:
  856.3 57.2 all-reduce.8
  916.6 38.3 all-reduce.10
  1235.3 39.1 all-reduce.14
  1277.4 56.5 all-reduce.12
where the time goes:
time: 1380 us; the launch traced here: 1370 us
  other arithmetic  901 us (65%)
  matrix products  172 us (12%)
  local copies, waits for them, and re-layouts  153 us (11%)
  waiting for transfers between devices  116 us (8%)
  between operations  14.3 us (1%)
    convert_element_type x2, other arithmetic, local(): extrap.reshape(chans * rows_here, extent).astype(jnp.bfloat16)  274 us
    dot_general x2, other arithmetic, local(): jnp.dot(extrap.reshape(chans * rows_here, extent).astype(jnp.bfloat16), t...  274 us
    scatter-add x2, other arithmetic, spread_all(): empty.at[flat_index.reshape(-1)].add(contrib.reshape(-1, 2, tile_side))  243 us
    psum x2, waiting for transfers between devices, local(): total = lax.psum(local_sum, 'chan')  99 us
    dot_general x2, matrix products, local(): lax.dot_general(grid_adj, table, (((1,), (1,)), ((), ())), preferred_elem...  69 us
    dot_general x2, matrix products, local(): jnp.dot(extrap.reshape(chans * rows_here, extent).astype(jnp.bfloat16), t...  45.8 us
    dot_general x2, matrix products, measure_all(): jnp.einsum('cbkrg,cbkvg->cbrv', picked, tiles, preferred_element_type=jnp...  30.8 us
    mul x2, other arithmetic, local(): pushed * jnp.minimum(1.0, radius[None, None, :, None] / norms[None])  29.2 us
  transfers between devices with their start and end apart: 8, of which 4 were waited for; matrix products, arithmetic and copies ran while one was open for 76% of the time, Pallas kernels for 0%

commit v1 on v0

v1 whole, which is shorter than its diff:
```python
import functools
import math

import jax
import jax.numpy as jnp
import ml_dtypes
import numpy as np
from jax import lax
from jax.experimental import pallas as pl
from jax.experimental.pallas import tpu as pltpu
from jax.sharding import PartitionSpec as P

ITERS = 2

STEP_PRIMAL = 0.5
STEP_PRIOR = 0.5
STEP_DATA = 1.0
RADIUS = 12.0
ROOT_HALF = 0.7071067811865476

GROUP = 8
RING = 32
CHUNK = 128
PIECE = 512


def shifted(shard, axis, by):
    count = lax.axis_size(axis)
    pairs = [(i, i + by) for i in range(count) if 0 <= i + by < count]
    return lax.ppermute(shard, axis, pairs)


def split_divide(value, by):
    if by & (by - 1) == 0:
        return lax.shift_right_logical(value, by.bit_length() - 1), value & (by - 1)
    return value // by, value % by


def transform_tables(extent, tile):
    j = np.arange(extent, dtype=np.int64)
    g = np.arange(tile, dtype=np.int64)
    angle = (g[:, None] * j[None, :] % extent) * (2.0 * math.pi / extent)
    cos, sin = np.cos(angle) / math.sqrt(extent), np.sin(angle) / math.sqrt(extent)
    adjoint = np.concatenate(
        [np.concatenate([cos, sin], 1), np.concatenate([-sin, cos], 1)], 0
    )
    forward = np.concatenate(
        [np.concatenate([cos.T, -sin.T], 1), np.concatenate([-sin.T, -cos.T], 1)], 0
    )
    high = forward.astype(ml_dtypes.bfloat16)
    low = (forward - high.astype(np.float64)).astype(ml_dtypes.bfloat16)
    blocks = extent // tile
    turn = (np.arange(blocks)[:, None] * np.arange(tile)[None, :] % blocks) * (2.0 * math.pi / blocks)
    return (
        adjoint.astype(ml_dtypes.bfloat16),
        high,
        low,
        np.cos(turn).astype(np.float32),
        np.sin(turn).astype(np.float32),
    )


def iteration_kernel(first, dims, *refs):
    chans, slots, blocks_per, rows, extent, tile = dims
    per_row = extent // tile
    cap = chans * slots * blocks_per
    refs = list(refs)
    ent, off = refs[:2]
    v_ref, tiles_ref, x_ref, u_ref, carry_ref = refs[2:7]
    refs = refs[7:]
    if not first:
        last_ref, tot_ref, rad_ref = refs[:3]
        refs = refs[3:]
    adj_ref, hi_ref, lo_ref, cos_ref, sin_ref = refs[:5]
    img_ref, push_ref, sum_ref, seen_ref, ef_ref, el_ref, pl_ref = refs[5:12]
    big, g_re, g_im, ph_c, ph_s, bacc, ebuf, tbuf, sems = refs[12:21]
    if not first:
        us, scale = refs[21:23]
    c = pl.program_id(0)
    total = off[chans]
    groups = lax.shift_right_logical(total + (GROUP - 1), GROUP.bit_length() - 1)
    chunks = lax.shift_right_logical(total + (CHUNK - 1), CHUNK.bit_length() - 1)

    def entry(q):
        where_it_goes, source = split_divide(ent[q], cap)
        row, block = split_divide(where_it_goes, per_row)
        return source, row, block

    def issue(group):
        slot = lax.rem(group, RING)
        for t in range(GROUP):
            source, _, _ = entry(group * GROUP + t)
            pltpu.make_async_copy(
                tiles_ref.at[source], tbuf.at[slot * GROUP + t], sems.at[slot]
            ).start()

    def await_group(group):
        slot = lax.rem(group, RING)
        pltpu.make_async_copy(
            tiles_ref.at[pl.ds(0, GROUP)], tbuf.at[pl.ds(slot * GROUP, GROUP)], sems.at[slot]
        ).wait()
        return slot * GROUP

    def prime():
        @pl.loop(0, jnp.minimum(groups, RING))
        def _(group):
            issue(group)

    def widen(value):
        return jnp.concatenate([value] * (PIECE // tile), axis=1)

    @pl.when(c == 0)
    def _():
        prime()
        sum_ref[...] = jnp.zeros_like(sum_ref)
        if not first:
            for band in range(2):
                for r in range(0, rows, 8):
                    norms = jnp.sqrt(tot_ref[band, r : r + 8] + 1e-06)
                    scale[band, r : r + 8] = jnp.minimum(1.0, rad_ref[r : r + 8] / norms)

        @pl.loop(0, groups)
        def _(group):
            base = await_group(group)
            re, im, co, si = [], [], [], []
            for t in range(GROUP):
                source, _, block = entry(group * GROUP + t)
                place, _ = split_divide(source, blocks_per)
                weights = v_ref[place].astype(jnp.bfloat16)
                contrib = jnp.dot(weights, tbuf[base + t], preferred_element_type=jnp.float32)
                re.append(contrib[0:1])
                im.append(contrib[1:2])
                co.append(cos_ref[pl.ds(block, 1), :])
                si.append(sin_ref[pl.ds(block, 1), :])
            at = pl.ds(pl.multiple_of(group * GROUP, GROUP), GROUP)
            g_re[at, :] = jnp.concatenate(re, axis=0)
            g_im[at, :] = jnp.concatenate(im, axis=0)
            ph_c[at, :] = jnp.concatenate(co, axis=0)
            ph_s[at, :] = jnp.concatenate(si, axis=0)

            @pl.when(group + RING < groups)
            def _():
                issue(group + RING)

        @pl.loop(0, chunks)
        def _(chunk):
            at = pl.ds(pl.multiple_of(chunk * CHUNK, CHUNK), CHUNK)
            lhs = jnp.concatenate([g_re[at, :], g_im[at, :]], axis=1).astype(jnp.bfloat16)
            turn_c, turn_s = widen(ph_c[at, :]), widen(ph_s[at, :])
            for j in range(0, extent, PIECE):
                even = jnp.dot(lhs, adj_ref[:, j : j + PIECE], preferred_element_type=jnp.float32)
                odd = jnp.dot(
                    lhs,
                    adj_ref[:, extent + j : extent + j + PIECE],
                    preferred_element_type=jnp.float32,
                )
                big[at, j : j + PIECE] = turn_c * even - turn_s * odd

        prime()

    start, end = off[c], off[c + 1]
    bacc[...] = jnp.zeros_like(bacc)

    @pl.loop(start, end)
    def _(q):
        _, row, _ = entry(q)
        bacc[pl.ds(row, 1), :] += big[pl.ds(q, 1), :]

    if not first:
        us[0, 7:8] = carry_ref[pl.ds(c, 1), :]
        for band in range(2):
            for r in range(0, rows, 8):
                value = u_ref[0, band, r : r + 8]
                if band == 0 and r == rows - 8:
                    value = jnp.concatenate([value[:7], last_ref[pl.ds(c, 1), :]], axis=0)
                us[band, r + 8 : r + 16] = value * scale[band, r : r + 8]

    def dual(band, r):
        return u_ref[0, band, r : r + 8] if first else us[band, r + 8 : r + 16]

    def dual_above(r):
        if not first:
            return us[0, r + 7 : r + 15]
        if r:
            return u_ref[0, 0, r - 1 : r + 7]
        return jnp.concatenate([carry_ref[pl.ds(c, 1), :], u_ref[0, 0, 0:7]], axis=0)

    column = lax.broadcasted_iota(jnp.int32, (8, extent), 1)
    for r in range(0, rows, 8):
        across = dual(1, r)
        leftward = jnp.where(column == 0, 0.0, pltpu.roll(across, 1, 1))
        synthesis = (dual_above(r) - dual(0, r) + leftward - across) * ROOT_HALF
        image = x_ref[0, r : r + 8]
        image_next = jnp.maximum(image - STEP_PRIMAL * (synthesis + bacc[r : r + 8]), 0.0)
        img_ref[0, r : r + 8] = image_next
        ebuf[r : r + 8] = 2.0 * image_next - image
    ebuf[rows : rows + 8] = jnp.zeros((8, extent), jnp.float32)

    @pl.loop(start, end)
    def _(q):
        _, row, _ = entry(q)
        big[pl.ds(q, 1), :] = ebuf[pl.ds(row, 1), :]

    for r in range(0, rows, 8):
        here = ebuf[r : r + 8]
        below = ebuf[r + 1 : r + 9]
        right = jnp.where(column == extent - 1, 0.0, pltpu.roll(here, extent - 1, 1))
        vertical = dual(0, r) + (STEP_PRIOR * ROOT_HALF) * (below - here)
        horizontal = dual(1, r) + (STEP_PRIOR * ROOT_HALF) * (right - here)
        push_ref[0, 0, r : r + 8] = vertical
        push_ref[0, 1, r : r + 8] = horizontal
        sum_ref[0, r : r + 8] += vertical * vertical
        sum_ref[1, r : r + 8] += horizontal * horizontal
        if r == rows - 8:
            pl_ref[pl.ds(c, 1), :] = vertical[7:8]
    ef_ref[pl.ds(c, 1), :] = ebuf[0:1]
    el_ref[pl.ds(c, 1), :] = ebuf[rows - 1 : rows]

    @pl.when(c == chans - 1)
    def _():
        seen_ref[...] = jnp.zeros_like(seen_ref)

        @pl.loop(0, chunks)
        def _(chunk):
            at = pl.ds(pl.multiple_of(chunk * CHUNK, CHUNK), CHUNK)
            turn_c, turn_s = widen(ph_c[at, :]), widen(ph_s[at, :])
            grid = jnp.zeros((CHUNK, 2 * tile), jnp.float32)
            for j in range(0, extent, PIECE):
                value = big[at, j : j + PIECE].astype(jnp.bfloat16).astype(jnp.float32)
                for turn, base in ((turn_c, j), (turn_s, extent + j)):
                    turned = value * turn
                    high = turned.astype(jnp.bfloat16)
                    low = (turned - high.astype(jnp.float32)).astype(jnp.bfloat16)
                    table = hi_ref[base : base + PIECE, :]
                    grid += jnp.dot(high, table, preferred_element_type=jnp.float32)
                    grid += jnp.dot(low, table, preferred_element_type=jnp.float32)
                    grid += jnp.dot(
                        high, lo_ref[base : base + PIECE, :], preferred_element_type=jnp.float32
                    )
            g_re[at, :] = grid[:, :tile]
            g_im[at, :] = grid[:, tile:]

        @pl.loop(0, groups)
        def _(group):
            base = await_group(group)
            at = pl.ds(pl.multiple_of(group * GROUP, GROUP), GROUP)
            lhs = jnp.concatenate([g_re[at, :], g_im[at, :]], axis=0).astype(jnp.bfloat16)
            for t in range(GROUP):
                q = group * GROUP + t
                source, _, _ = entry(q)
                place, _ = split_divide(source, blocks_per)
                part = lax.dot_general(
                    lhs, tbuf[base + t], (((1,), (1,)), ((), ())), preferred_element_type=jnp.float32
                )
                part = jnp.concatenate([part[t : t + 1], part[GROUP + t : GROUP + t + 1]], axis=0)
                seen_ref[place] += jnp.where(q < total, part, 0.0)

            @pl.when(group + RING < groups)
            def _():
                issue(group + RING)


def iteration(first, tables, ent, off, v, tiles, x, u, carry, extra=()):
    chans, rows, extent = x.shape
    tile = tiles.shape[-1]
    slots = v.shape[0] // chans
    blocks_per = tiles.shape[0] // v.shape[0]
    cap = ent.shape[0]
    dims = (chans, slots, blocks_per, rows, extent, tile)

    def whole(shape):
        return pl.BlockSpec(shape, lambda c, *_: (0,) * len(shape), pipeline_mode=pl.Buffered(1))

    def per_channel(shape):
        return pl.BlockSpec((1,) + shape, lambda c, *_: (c,) + (0,) * len(shape))

    image_spec, dual_spec = per_channel((rows, extent)), per_channel((2, rows, extent))
    resident = lambda shape: jax.ShapeDtypeStruct(shape, jnp.float32)
    outs = [x.shape, u.shape, (2, rows, extent), v.shape] + [(chans, extent)] * 3
    rows_cap = max(cap, CHUNK)
    scratch = [
        pltpu.VMEM((rows_cap, extent), jnp.float32),
        pltpu.VMEM((rows_cap, tile), jnp.float32),
        pltpu.VMEM((rows_cap, tile), jnp.float32),
        pltpu.VMEM((rows_cap, tile), jnp.float32),
        pltpu.VMEM((rows_cap, tile), jnp.float32),
        pltpu.VMEM((rows, extent), jnp.float32),
        pltpu.VMEM((rows + 8, extent), jnp.float32),
        pltpu.VMEM((RING * GROUP, tile, tile), jnp.bfloat16),
        pltpu.SemaphoreType.DMA((RING,)),
    ]
    if not first:
        scratch += [
            pltpu.VMEM((2, rows + 8, extent), jnp.float32),
            pltpu.VMEM((2, rows, extent), jnp.float32),
        ]
    operands = [v, tiles, x, u, carry, *extra, *tables]
    in_specs = [whole(v.shape), pl.BlockSpec(memory_space=pl.ANY), image_spec, dual_spec]
    in_specs += [whole(a.shape) for a in operands[4:]]
    return pl.pallas_call(
        functools.partial(iteration_kernel, first, dims),
        out_shape=[resident(s) for s in outs],
        grid_spec=pltpu.PrefetchScalarGridSpec(
            num_scalar_prefetch=2,
            grid=(chans,),
            in_specs=in_specs,
            out_specs=[image_spec, dual_spec] + [whole(s) for s in outs[2:]],
            scratch_shapes=scratch,
        ),
        compiler_params=pltpu.CompilerParams(
            dimension_semantics=("arbitrary",), vmem_limit_bytes=58 << 20
        ),
        name="primal_dual_first" if first else "primal_dual_next",
    )(ent, off, *operands)


def shrink_kernel(push_ref, last_ref, tot_ref, rad_ref, out_ref, scale):
    rows = push_ref.shape[2]
    c = pl.program_id(0)

    @pl.when(c == 0)
    def _():
        for band in range(2):
            for r in range(0, rows, 8):
                norms = jnp.sqrt(tot_ref[band, r : r + 8] + 1e-06)
                scale[band, r : r + 8] = jnp.minimum(1.0, rad_ref[r : r + 8] / norms)

    for band in range(2):
        for r in range(0, rows, 8):
            value = push_ref[0, band, r : r + 8]
            if band == 0 and r == rows - 8:
                value = jnp.concatenate([value[:7], last_ref[pl.ds(c, 1), :]], axis=0)
            out_ref[0, band, r : r + 8] = value * scale[band, r : r + 8]


def shrink(push, last, total, radius):
    chans, _, rows, extent = push.shape

    def whole(shape):
        return pl.BlockSpec(shape, lambda c: (0,) * len(shape), pipeline_mode=pl.Buffered(1))

    dual_spec = pl.BlockSpec((1, 2, rows, extent), lambda c: (c, 0, 0, 0))
    return pl.pallas_call(
        shrink_kernel,
        out_shape=jax.ShapeDtypeStruct(push.shape, jnp.float32),
        grid=(chans,),
        in_specs=[dual_spec, whole(last.shape), whole(total.shape), whole(radius.shape)],
        out_specs=dual_spec,
        scratch_shapes=[pltpu.VMEM((2, rows, extent), jnp.float32)],
        compiler_params=pltpu.CompilerParams(
            dimension_semantics=("arbitrary",), vmem_limit_bytes=32 << 20
        ),
        name="shrink",
    )(push, last, total, radius)


def exchange(value, axis, bit):
    count = lax.axis_size(axis)
    return lax.ppermute(value, axis, [(i, i ^ bit) for i in range(count)])


def halve(value, axis, bits):
    index = lax.axis_index(axis)
    for bit in bits:
        half = value.shape[0] // 2
        mine = (index // bit) % 2
        keep = lax.dynamic_slice_in_dim(value, mine * half, half, 0)
        send = lax.dynamic_slice_in_dim(value, (1 - mine) * half, half, 0)
        value = keep + exchange(send, axis, bit)
    return value


def double(value, axis, bits):
    index = lax.axis_index(axis)
    for bit in reversed(bits):
        other = exchange(value, axis, bit)
        first = (index // bit) % 2 == 0
        value = jnp.concatenate(
            [jnp.where(first, value, other), jnp.where(first, other, value)], axis=0
        )
    return value


def shard_of(value, axis, bits):
    index = lax.axis_index(axis)
    for bit in bits:
        half = value.shape[0] // 2
        value = lax.dynamic_slice_in_dim(value, ((index // bit) % 2) * half, half, 0)
    return value


def chan_orders(count):
    bits = [1 << k for k in range(count.bit_length() - 1)]
    inner, outer = bits[:1], bits[1:]
    half = len(outer) // 2
    return inner + outer[:half] + outer[half:], inner + outer[half:] + outer[:half]


def sum_over_channels(local_sum):
    count = lax.axis_size("chan")
    if count & (count - 1) or local_sum.shape[1] % count:
        return lax.psum(local_sum, "chan")
    order_a, order_b = chan_orders(count)
    vertical, horizontal = local_sum[0], local_sum[1]
    vertical = double(halve(vertical, "chan", order_a), "chan", order_a)
    horizontal = double(halve(horizontal, "chan", order_b), "chan", order_b)
    return jnp.stack([vertical, horizontal])


def update_data(seen, data_dual, observed, live):
    count = lax.axis_size("facet")
    if count & (count - 1) or seen.shape[0] % count:
        seen = lax.psum(seen, "facet")
        return (data_dual + STEP_DATA * (seen - observed)) * live / (1.0 + STEP_DATA)
    bits = [1 << k for k in range(count.bit_length() - 1)]
    seen = halve(seen, "facet", bits)
    data_dual, observed, live = (shard_of(a, "facet", bits) for a in (data_dual, observed, live))
    fresh = (data_dual + STEP_DATA * (seen - observed)) * live / (1.0 + STEP_DATA)
    return double(fresh, "facet", bits)


def local(x_init, u_init, v_init, observed, tiles, pattern, counts, facet_bounds):
    chans, rows, extent = x_init.shape
    slots, blocks_per = pattern.shape[1:]
    tile = tiles.shape[-1]
    per_row = extent // tile
    facet = lax.axis_index("facet")
    row_start = facet * rows
    cap = chans * slots * blocks_per
    tables = [jnp.asarray(t) for t in transform_tables(extent, tile)]

    live = jnp.arange(slots, dtype=jnp.int32)[None, :] < counts[:, None]
    local_index = pattern - row_start * per_row
    keep = (local_index >= 0) & (local_index < rows * per_row) & live[:, :, None]
    keep = keep.reshape(cap)
    order = jnp.arange(cap, dtype=jnp.int32)
    ahead = jnp.sum(
        (keep[None, :] & (order[None, :] < order[:, None])).astype(jnp.int32), axis=1
    )
    packed = jnp.where(keep, local_index.reshape(cap) * cap + order, 0)
    ent = jnp.sum(
        jnp.where(keep[None, :] & (ahead[None, :] == order[:, None]), packed[None, :], 0), axis=1
    )
    kept = jnp.sum(keep.reshape(chans, -1).astype(jnp.int32), axis=1)
    edges = jnp.arange(chans + 1, dtype=jnp.int32)
    off = jnp.sum(jnp.where(edges[None, :chans] < edges[:, None], kept[None, :], 0), axis=1)

    row_ids = row_start - 1 + jnp.arange(rows + 1, dtype=jnp.int32)
    inside = (row_ids[None, :] >= facet_bounds[:, 0:1]) & (row_ids[None, :] < facet_bounds[:, 1:2])
    cover = jnp.sum(inside.astype(jnp.float32), axis=0)
    radius = (RADIUS / cover)[:, None]
    radius, radius_above = radius[1:], radius[0]

    live_float = jnp.broadcast_to(live.reshape(-1, 1, 1).astype(jnp.float32), (chans * slots, 1, 1))
    observed = observed.reshape(chans * slots, 2, tile)
    data_dual = v_init.reshape(chans * slots, 2, tile)
    tiles = tiles.reshape(cap, tile, tile)
    image, dual = x_init, u_init
    carry = shifted(u_init[:, 0, -1, :], "facet", 1)
    extra = ()
    for rounds in range(ITERS):
        image, dual, local_sum, seen, first_row, last_row, pushed_last = iteration(
            rounds == 0, tables, ent, off, data_dual, tiles, image, dual, carry, extra
        )
        half_step = STEP_PRIOR * ROOT_HALF
        pushed_last = pushed_last + half_step * shifted(first_row, "facet", -1)
        local_sum = lax.dynamic_update_slice(
            local_sum, jnp.sum(pushed_last * pushed_last, axis=0)[None, None], (0, rows - 1, 0)
        )
        total = sum_over_channels(local_sum)
        data_dual = update_data(seen, data_dual, observed, live_float)
        extra = (pushed_last, total, radius)
        if rounds + 1 < ITERS:
            above = carry + half_step * (first_row - shifted(last_row, "facet", 1))
            norms = jnp.sqrt(shifted(total[0, rows - 1 :], "facet", 1) + 1e-06)
            carry = jnp.where(facet > 0, above * jnp.minimum(1.0, radius_above / norms), 0.0)
    return (
        image,
        shrink(dual, *extra),
        data_dual.reshape(v_init.shape),
    )


def solution(mesh):
    in_specs = (
        P("chan", "facet", None),
        P("chan", None, "facet", None),
        P("chan", None, None, None),
        P("chan", None, None, None),
        P("chan", None, None, None, None),
        P("chan", None, None),
        P("chan"),
        P(),
    )
    out_specs = (
        P("chan", "facet", None),
        P("chan", None, "facet", None),
        P("chan", None, None, None),
    )
    return jax.shard_map(local, mesh=mesh, in_specs=in_specs, out_specs=out_specs, check_vma=False)
```

time: 1380 us -> 233 us (0.17)
  other arithmetic: 901 us -> 14.9 us
  matrix products: 172 us -> 0 us
  local copies, waits for them, and re-layouts: 153 us -> 12.3 us
  waiting for transfers between devices: 116 us -> 20.6 us
  starting transfers between devices: 10.9 us -> 95.8 us
  Pallas kernels: 0 us -> 84 us
    convert_element_type x5 -> x1, other arithmetic: 294 us -> 0.73 us  [local(): live.reshape(-1, 1, 1).astype(jnp.float32)]
    dot_general x2 -> x0, other arithmetic: 274 us -> none  [local(): jnp.dot(extrap.reshape(chans * rows_here, extent).astype(jnp.bfloat16), t...]
    scatter-add x2 -> x0, other arithmetic: 243 us -> none  [spread_all(): empty.at[flat_index.reshape(-1)].add(contrib.reshape(-1, 2, tile_side))]
    dot_general x8 -> x0, matrix products: 172 us -> none  [the longest x2 69 us: local(): lax.dot_general(grid_adj, table, (((1,), (1,)), ((), ())), preferred_elem...]
    psum x4 -> x0, waiting for transfers between devices: 116 us -> none  [the longest x2 99 us: local(): total = lax.psum(local_sum, 'chan')]
    pallas_call x0 -> x3, Pallas kernels: none -> 84 us  [the longest x2 74.6 us: iteration(): pl.pallas_call(functools.partial(iteration_kernel, first, dims), out_shap...]
    ppermute x0 -> x32, starting transfers between devices: none -> 79.3 us  [exchange(): return lax.ppermute(value, axis, [(i, i ^ bit) for i in range(count)])]
    mul x3 -> x0, other arithmetic: 29.2 us -> none  [the longest x2 29.2 us: local(): pushed * jnp.minimum(1.0, radius[None, None, :, None] / norms[None])]
  transfers between devices with their start and end apart: 8 -> 37, of which waited for: 4 -> 12; matrix products, arithmetic and copies ran while one was open for 76% -> 11% of each run, Pallas kernels for 0% -> 0%
where the time goes in v1:
time: 233 us; the launch traced here: 229 us
  starting transfers between devices  95.8 us (41%)
  Pallas kernels  84 us (36%)
  waiting for transfers between devices  20.6 us (9%)
  other arithmetic  14.9 us (6%)
  local copies, waits for them, and re-layouts  12.3 us (5%)
    ppermute x32, starting transfers between devices, exchange(): return lax.ppermute(value, axis, [(i, i ^ bit) for i in range(count)])  79.3 us
    pallas_call x2, Pallas kernels, iteration(): pl.pallas_call(functools.partial(iteration_kernel, first, dims), out_shap...  74.6 us
    ppermute x32, waiting for transfers between devices, exchange(): return lax.ppermute(value, axis, [(i, i ^ bit) for i in range(count)])  17.1 us
    ppermute x5, starting transfers between devices, shifted(): return lax.ppermute(shard, axis, pairs)  16.6 us
    pallas_call x1, Pallas kernels, shrink(): pl.pallas_call(shrink_kernel, out_shape=jax.ShapeDtypeStruct(push.shape,...  9.42 us
  transfers between devices with their start and end apart: 37, of which 12 were waited for; matrix products, arithmetic and copies ran while one was open for 11% of the time, Pallas kernels for 0%

profile of v1, /device:TPU:0, one launch (start us, length us, event | category | flops | bytes accessed | tf_op | source)
XLA Modules:
  0.0 229.0 jit_solution(3834811023492674276)
XLA Ops:
  2.0 4.9 %collective-permute-start = (f32[16,2048]{1,0:T(8,128)S(1)}, f32[16,2048]{1,0:T(8,128)S(1)}, u32[]{:S(2)}, u32[]{:S(2)}) collective-permute-start(f32[16,2048]{1,0:T(8,128)S(1)} %bitcast.74), channel_id=1, source_target_pairs={{0,1},{1,2},{2,3},{4,5},{5,6},{6,7},{8,9},{9,10},{10,11},{12,13},{... | collective-permute-start | bytes 393224 | tf_op jit(solution)/shard_map/ppermute | solution.py:30
  10.7 1.5 select_reduce_fusion.refs_0_
  13.6 37.2 %primal_dual_first.1 = (f32[16,64,2048]{2,1,0:T(8,128)}, f32[16,2,64,2048]{3,2,1,0:T(8,128)}, f32[2,64,2048]{2,1,0:T(8,128)}, f32[512,2,128]{2,1,0:T(2,128)}, f3...) custom-call(s32[1024]{0:T(1024)} %select_reduce_fusion.refs_0_, s32[17]{0:T(128)} %select_reduce_fusion.1.refs_1_, ...), custom_call_target="tpu_custom_call" | custom-call | tf_op jit(solution)/shard_map/primal_dual_first/pallas_call | solution.py:300
  53.0 4.7 %collective-permute-start.5 = (f32[16,2048]{1,0:T(8,128)}, f32[16,2048]{1,0:T(8,128)S(1)}, u32[]{:S(2)}, u32[]{:S(2)}) collective-permute-start(f32[16,2048]{1,0:T(8,128)} %get-tuple-element.20), channel_id=1, source_target_pairs={{0,1},{1,2},{2,3},{4,5},{5,6},{6,7},{8,9},{9,10},{10,11},{12,13},{... | collective-permute-start | bytes 393224 | tf_op jit(solution)/shard_map/ppermute | solution.py:30
  58.7 2.1 collective-permute-start.1
  60.8 1.6 multiply_reduce_fusion.1
  62.4 1.5 dynamic_update_slice.6
  66.5 1.9 collective-permute-start.2
  68.6 7.0 %collective-permute-done.2 = f32[128,2,128]{2,1,0:T(2,128)S(1)} collective-permute-done((f32[128,2,128]{2,1,0:T(2,128)S(1)}, f32[128,2,128]{2,1,0:T(2,128)S(1)}, u32[]{:S(2)}, u32[]{:S(2)}) %collective-permute-start.2) | collective-permute-done | bytes 131104 | tf_op jit(solution)/shard_map/ppermute | solution.py:359
  77.4 19.3 %collective-permute-start.15 = (f32[16,2048]{1,0:T(8,128)S(1)}, f32[16,2048]{1,0:T(8,128)S(1)}, u32[]{:S(2)}, u32[]{:S(2)}) collective-permute-start(f32[16,2048]{1,0:T(8,128)S(1)} %constant_dynamic-slice_fusion.6), channel_id=1, source_target_pairs={{0,16},{4,20},{8,24},{12,28},{16,0},{20,4},{24,8},{28,12},{1,17},{... | collective-permute-start | bytes 393224 | tf_op jit(solution)/shard_map/ppermute | solution.py:359
  96.9 1.9 collective-permute-start.4
  99.9 3.1 %collective-permute-start.16 = (f32[8,2048]{1,0:T(8,128)S(1)}, f32[8,2048]{1,0:T(8,128)S(1)}, u32[]{:S(2)}, u32[]{:S(2)}) collective-permute-start(f32[8,2048]{1,0:T(8,128)S(1)} %constant_dynamic-slice_fusion.5), channel_id=1, source_target_pairs={{0,8},{4,12},{8,0},{12,4},{16,24},{20,28},{24,16},{28,20},{1,9},{5... | collective-permute-start | bytes 196616 | tf_op jit(solution)/shard_map/ppermute | solution.py:359
  105.3 2.5 %collective-permute-start.17 = (f32[8,2048]{1,0:T(8,128)S(1)}, f32[8,2048]{1,0:T(8,128)S(1)}, u32[]{:S(2)}, u32[]{:S(2)}) collective-permute-start(f32[8,2048]{1,0:T(8,128)S(1)} %dynamic-slice_add_fusion.8), channel_id=1, source_target_pairs={{0,8},{4,12},{8,0},{12,4},{16,24},{20,28},{24,16},{28,20},{1,9},{5... | collective-permute-start | bytes 196616 | tf_op jit(solution)/shard_map/ppermute | solution.py:359
  108.6 1.8 collective-permute-start.11
  111.8 1.8 collective-permute-done.11
  113.8 1.7 collective-permute-done.18
  116.9 4.1 %collective-permute-start.13 = (f32[1,2048]{1,0:T(1,128)S(1)}, f32[1,2048]{1,0:T(1,128)S(1)}, u32[]{:S(2)}, u32[]{:S(2)}) collective-permute-start(f32[1,2048]{1,0:T(1,128)S(1)} %slice_bitcast_fusion), channel_id=1, source_target_pairs={{0,1},{1,2},{2,3},{4,5},{5,6},{6,7},{8,9},{9,10},{10,11},{12,13},{... | collective-permute-start | bytes 24584 | tf_op jit(solution)/shard_map/ppermute | solution.py:30
  123.0 37.4 %primal_dual_next.1 = (f32[16,64,2048]{2,1,0:T(8,128)}, f32[16,2,64,2048]{3,2,1,0:T(8,128)}, f32[2,64,2048]{2,1,0:T(8,128)}, f32[512,2,128]{2,1,0:T(2,128)}, f32...) custom-call(s32[1024]{0:T(1024)} %select_reduce_fusion.refs_0_, s32[17]{0:T(128)} %select_reduce_fusion.1.refs_1_, ...), custom_call_target="tpu_custom_call" | custom-call | tf_op jit(solution)/shard_map/primal_dual_next/pallas_call | solution.py:300
  162.8 3.7 %collective-permute-start.33 = (f32[256,2,128]{2,1,0:T(2,128)S(1)}, f32[256,2,128]{2,1,0:T(2,128)S(1)}, u32[]{:S(2)}, u32[]{:S(2)}) collective-permute-start(f32[256,2,128]{2,1,0:T(2,128)S(1)} %constant_dynamic-slice_fusion.12), channel_id=1, source_target_pairs={{0,1},{1,0},{2,3},{3,2},{4,5},{5,4},{6,7},{7,6},{8,9},{9,8},{10,11... | collective-permute-start | bytes 786440 | tf_op jit(solution)/shard_map/ppermute | solution.py:359
  166.5 3.6 %collective-permute-done.20 = f32[16,2048]{1,0:T(8,128)S(1)} collective-permute-done((f32[16,2048]{1,0:T(8,128)}, f32[16,2048]{1,0:T(8,128)S(1)}, u32[]{:S(2)}, u32[]{:S(2)}) %collective-permute-start.20) | collective-permute-done | bytes 131104 | tf_op jit(solution)/shard_map/ppermute | solution.py:30
  171.0 1.5 dynamic_update_slice.7
  174.7 2.1 collective-permute-start.34
  176.8 1.5 collective-permute-start.28
  178.4 17.3 %collective-permute-start.22 = (f32[16,2048]{1,0:T(8,128)S(1)}, f32[16,2048]{1,0:T(8,128)S(1)}, u32[]{:S(2)}, u32[]{:S(2)}) collective-permute-start(f32[16,2048]{1,0:T(8,128)S(1)} %constant_dynamic-slice_fusion.4), channel_id=1, source_target_pairs={{0,8},{4,12},{8,0},{12,4},{16,24},{20,28},{24,16},{28,20},{1,9},{5... | collective-permute-start | bytes 393224 | tf_op jit(solution)/shard_map/ppermute | solution.py:359
  196.9 2.2 collective-permute-start.29
  199.2 3.5 %collective-permute-start.23 = (f32[8,2048]{1,0:T(8,128)S(1)}, f32[8,2048]{1,0:T(8,128)S(1)}, u32[]{:S(2)}, u32[]{:S(2)}) collective-permute-start(f32[8,2048]{1,0:T(8,128)S(1)} %constant_dynamic-slice_fusion.3), channel_id=1, source_target_pairs={{0,16},{4,20},{8,24},{12,28},{16,0},{20,4},{24,8},{28,12},{1,17},{... | collective-permute-start | bytes 196616 | tf_op jit(solution)/shard_map/ppermute | solution.py:359
  205.3 5.0 %collective-permute-start.24 = (f32[8,2048]{1,0:T(8,128)S(1)}, f32[8,2048]{1,0:T(8,128)S(1)}, u32[]{:S(2)}, u32[]{:S(2)}) collective-permute-start(f32[8,2048]{1,0:T(8,128)S(1)} %dynamic-slice_add_fusion.7), channel_id=1, source_target_pairs={{0,16},{4,20},{8,24},{12,28},{16,0},{20,4},{24,8},{28,12},{1,17},{... | collective-permute-start | bytes 196616 | tf_op jit(solution)/shard_map/ppermute | solution.py:359
  210.4 2.3 collective-permute-start.31
  212.7 2.1 collective-permute-start.25
  216.1 1.6 collective-permute-done.25
  217.9 1.5 collective-permute-done.26
  219.6 9.4 %shrink.1 = f32[16,2,64,2048]{3,2,1,0:T(8,128)} custom-call(f32[16,2,64,2048]{3,2,1,0:T(8,128)S(1)} %copy-done, f32[16,2048]{1,0:T(8,128)S(1)} %get-tuple-element.30.last_ref, f32[2,64,2048]{2,1,0:T(8,128)S(1)} %pad_maximum_fusion.1.tot_ref, f32[64,1]{1,0:T(8,128)S(1)} %copy-done.1), custom_call_target="tpu_custom_call" | custom-call | tf_op jit(solution)/shard_map/shrink/pallas_call | solution.py:343
  (154 shorter events, 34.3 us)
Async XLA Ops:
  2.0 10.9 %collective-permute-start = (f32[16,2048]{1,0:T(8,128)S(1)}, f32[16,2048]{1,0:T(8,128)S(1)}, u32[]{:S(2)}, u32[]{:S(2)}) collective-permute-start(f32[16,2048]{1,0:T(8,128)S(1)} %bitcast.74), channel_id=1, source_target_pairs={{0,1},{1,2},{2,3},{4,5},{5,6},{6,7},{8,9},{9,10},{10,11},{12,13},{... | collective-permute-start | bytes 393224 | tf_op jit(solution)/shard_map/ppermute | solution.py:30
  50.8 10.1 %collective-permute-start.6 = (f32[16,2048]{1,0:T(8,128)}, f32[16,2048]{1,0:T(8,128)S(1)}, u32[]{:S(2)}, u32[]{:S(2)}) collective-permute-start(f32[16,2048]{1,0:T(8,128)} %get-tuple-element.19), channel_id=1, source_target_pairs={{1,0},{2,1},{3,2},{5,4},{6,5},{7,6},{9,8},{10,9},{11,10},{13,12},{... | collective-permute-start | bytes 393224 | tf_op jit(solution)/shard_map/ppermute | solution.py:30
  53.0 69.2 %collective-permute-start.5 = (f32[16,2048]{1,0:T(8,128)}, f32[16,2048]{1,0:T(8,128)S(1)}, u32[]{:S(2)}, u32[]{:S(2)}) collective-permute-start(f32[16,2048]{1,0:T(8,128)} %get-tuple-element.20), channel_id=1, source_target_pairs={{0,1},{1,2},{2,3},{4,5},{5,6},{6,7},{8,9},{9,10},{10,11},{12,13},{... | collective-permute-start | bytes 393224 | tf_op jit(solution)/shard_map/ppermute | solution.py:30
  58.7 6.7 %collective-permute-start.1 = (f32[256,2,128]{2,1,0:T(2,128)S(1)}, f32[256,2,128]{2,1,0:T(2,128)S(1)}, u32[]{:S(2)}, u32[]{:S(2)}) collective-permute-start(f32[256,2,128]{2,1,0:T(2,128)S(1)} %constant_dynamic-slice_fusion.11), channel_id=1, source_target_pairs={{0,1},{1,0},{2,3},{3,2},{4,5},{5,4},{6,7},{7,6},{8,9},{9,8},{10,11... | collective-permute-start | bytes 786440 | tf_op jit(solution)/shard_map/ppermute | solution.py:359
  65.2 11.6 %collective-permute-start.7 = (f32[32,2048]{1,0:T(8,128)S(1)}, f32[32,2048]{1,0:T(8,128)S(1)}, u32[]{:S(2)}, u32[]{:S(2)}) collective-permute-start(f32[32,2048]{1,0:T(8,128)S(1)} %dynamic-slice_bitcast_fusion.3), channel_id=1, source_target_pairs={{0,4},{4,0},{8,12},{12,8},{16,20},{20,16},{24,28},{28,24},{1,5},{5... | collective-permute-start | bytes 786440 | tf_op jit(solution)/shard_map/ppermute | solution.py:359
  66.5 9.0 %collective-permute-start.2 = (f32[128,2,128]{2,1,0:T(2,128)S(1)}, f32[128,2,128]{2,1,0:T(2,128)S(1)}, u32[]{:S(2)}, u32[]{:S(2)}) collective-permute-start(f32[128,2,128]{2,1,0:T(2,128)S(1)} %constant_dynamic-slice_fusion.10), channel_id=1, source_target_pairs={{0,2},{1,3},{2,0},{3,1},{4,6},{5,7},{6,4},{7,5},{8,10},{9,11},{10,... | collective-permute-start | bytes 393224 | tf_op jit(solution)/shard_map/ppermute | solution.py:359
  68.5 8.8 %collective-permute-start.14 = (f32[32,2048]{1,0:T(8,128)S(1)}, f32[32,2048]{1,0:T(8,128)S(1)}, u32[]{:S(2)}, u32[]{:S(2)}) collective-permute-start(f32[32,2048]{1,0:T(8,128)S(1)} %dynamic-slice_bitcast_fusion.2), channel_id=1, source_target_pairs={{0,4},{4,0},{8,12},{12,8},{16,20},{20,16},{24,28},{28,24},{1,5},{5... | collective-permute-start | bytes 786440 | tf_op jit(solution)/shard_map/ppermute | solution.py:359
  76.7 20.0 %collective-permute-start.3 = (f32[128,2,128]{2,1,0:T(2,128)S(1)}, f32[128,2,128]{2,1,0:T(2,128)S(1)}, u32[]{:S(2)}, u32[]{:S(2)}) collective-permute-start(f32[128,2,128]{2,1,0:T(2,128)S(1)} %multiply_multiply_fusion.1), channel_id=1, source_target_pairs={{0,2},{1,3},{2,0},{3,1},{4,6},{5,7},{6,4},{7,5},{8,10},{9,11},{10,... | collective-permute-start | bytes 393224 | tf_op jit(solution)/shard_map/ppermute | solution.py:359
  76.9 21.9 %collective-permute-start.8 = (f32[16,2048]{1,0:T(8,128)S(1)}, f32[16,2048]{1,0:T(8,128)S(1)}, u32[]{:S(2)}, u32[]{:S(2)}) collective-permute-start(f32[16,2048]{1,0:T(8,128)S(1)} %constant_dynamic-slice_fusion.8), channel_id=1, source_target_pairs={{0,8},{4,12},{8,0},{12,4},{16,24},{20,28},{24,16},{28,20},{1,9},{5... | collective-permute-start | bytes 393224 | tf_op jit(solution)/shard_map/ppermute | solution.py:359
  77.4 22.5 %collective-permute-start.15 = (f32[16,2048]{1,0:T(8,128)S(1)}, f32[16,2048]{1,0:T(8,128)S(1)}, u32[]{:S(2)}, u32[]{:S(2)}) collective-permute-start(f32[16,2048]{1,0:T(8,128)S(1)} %constant_dynamic-slice_fusion.6), channel_id=1, source_target_pairs={{0,16},{4,20},{8,24},{12,28},{16,0},{20,4},{24,8},{28,12},{1,17},{... | collective-permute-start | bytes 393224 | tf_op jit(solution)/shard_map/ppermute | solution.py:359
  96.9 18.7 %collective-permute-start.4 = (f32[256,2,128]{2,1,0:T(2,128)S(1)}, f32[256,2,128]{2,1,0:T(2,128)S(1)}, u32[]{:S(2)}, u32[]{:S(2)}) collective-permute-start(f32[256,2,128]{2,1,0:T(2,128)S(1)} %pad_maximum_fusion.4), channel_id=1, source_target_pairs={{0,1},{1,0},{2,3},{3,2},{4,5},{5,4},{6,7},{7,6},{8,9},{9,8},{10,11... | collective-permute-start | bytes 786440 | tf_op jit(solution)/shard_map/ppermute | solution.py:359
  98.9 4.7 %collective-permute-start.9 = (f32[8,2048]{1,0:T(8,128)S(1)}, f32[8,2048]{1,0:T(8,128)S(1)}, u32[]{:S(2)}, u32[]{:S(2)}) collective-permute-start(f32[8,2048]{1,0:T(8,128)S(1)} %constant_dynamic-slice_fusion.7), channel_id=1, source_target_pairs={{0,16},{4,20},{8,24},{12,28},{16,0},{20,4},{24,8},{28,12},{1,17},{... | collective-permute-start | bytes 196616 | tf_op jit(solution)/shard_map/ppermute | solution.py:359
  99.9 5.4 %collective-permute-start.16 = (f32[8,2048]{1,0:T(8,128)S(1)}, f32[8,2048]{1,0:T(8,128)S(1)}, u32[]{:S(2)}, u32[]{:S(2)}) collective-permute-start(f32[8,2048]{1,0:T(8,128)S(1)} %constant_dynamic-slice_fusion.5), channel_id=1, source_target_pairs={{0,8},{4,12},{8,0},{12,4},{16,24},{20,28},{24,16},{28,20},{1,9},{5... | collective-permute-start | bytes 196616 | tf_op jit(solution)/shard_map/ppermute | solution.py:359
  103.6 4.9 %collective-permute-start.10 = (f32[8,2048]{1,0:T(8,128)S(1)}, f32[8,2048]{1,0:T(8,128)S(1)}, u32[]{:S(2)}, u32[]{:S(2)}) collective-permute-start(f32[8,2048]{1,0:T(8,128)S(1)} %dynamic-slice_add_fusion.9), channel_id=1, source_target_pairs={{0,16},{4,20},{8,24},{12,28},{16,0},{20,4},{24,8},{28,12},{1,17},{... | collective-permute-start | bytes 196616 | tf_op jit(solution)/shard_map/ppermute | solution.py:359
  105.3 5.0 %collective-permute-start.17 = (f32[8,2048]{1,0:T(8,128)S(1)}, f32[8,2048]{1,0:T(8,128)S(1)}, u32[]{:S(2)}, u32[]{:S(2)}) collective-permute-start(f32[8,2048]{1,0:T(8,128)S(1)} %dynamic-slice_add_fusion.8), channel_id=1, source_target_pairs={{0,8},{4,12},{8,0},{12,4},{16,24},{20,28},{24,16},{28,20},{1,9},{5... | collective-permute-start | bytes 196616 | tf_op jit(solution)/shard_map/ppermute | solution.py:359
  108.6 5.0 %collective-permute-start.11 = (f32[16,2048]{1,0:T(8,128)S(1)}, f32[16,2048]{1,0:T(8,128)S(1)}, u32[]{:S(2)}, u32[]{:S(2)}) collective-permute-start(f32[16,2048]{1,0:T(8,128)S(1)} %pad_maximum_fusion.10), channel_id=1, source_target_pairs={{0,8},{4,12},{8,0},{12,4},{16,24},{20,28},{24,16},{28,20},{1,9},{5... | collective-permute-start | bytes 393224 | tf_op jit(solution)/shard_map/ppermute | solution.py:359
  110.4 5.0 %collective-permute-start.18 = (f32[16,2048]{1,0:T(8,128)S(1)}, f32[16,2048]{1,0:T(8,128)S(1)}, u32[]{:S(2)}, u32[]{:S(2)}) collective-permute-start(f32[16,2048]{1,0:T(8,128)S(1)} %pad_maximum_fusion.11), channel_id=1, source_target_pairs={{0,16},{4,20},{8,24},{12,28},{16,0},{20,4},{24,8},{28,12},{1,17},{... | collective-permute-start | bytes 393224 | tf_op jit(solution)/shard_map/ppermute | solution.py:359
  115.5 5.5 %collective-permute-start.19 = (f32[32,2048]{1,0:T(8,128)S(1)}, f32[32,2048]{1,0:T(8,128)S(1)}, u32[]{:S(2)}, u32[]{:S(2)}) collective-permute-start(f32[32,2048]{1,0:T(8,128)S(1)} %pad_maximum_fusion.6), channel_id=1, source_target_pairs={{0,4},{4,0},{8,12},{12,8},{16,20},{20,16},{24,28},{28,24},{1,5},{5... | collective-permute-start | bytes 786440 | tf_op jit(solution)/shard_map/ppermute | solution.py:359
  116.9 5.3 %collective-permute-start.13 = (f32[1,2048]{1,0:T(1,128)S(1)}, f32[1,2048]{1,0:T(1,128)S(1)}, u32[]{:S(2)}, u32[]{:S(2)}) collective-permute-start(f32[1,2048]{1,0:T(1,128)S(1)} %slice_bitcast_fusion), channel_id=1, source_target_pairs={{0,1},{1,2},{2,3},{4,5},{5,6},{6,7},{8,9},{9,10},{10,11},{12,13},{... | collective-permute-start | bytes 24584 | tf_op jit(solution)/shard_map/ppermute | solution.py:30
  160.4 9.7 %collective-permute-start.20 = (f32[16,2048]{1,0:T(8,128)}, f32[16,2048]{1,0:T(8,128)S(1)}, u32[]{:S(2)}, u32[]{:S(2)}) collective-permute-start(f32[16,2048]{1,0:T(8,128)} %get-tuple-element.26), channel_id=1, source_target_pairs={{1,0},{2,1},{3,2},{5,4},{6,5},{7,6},{9,8},{10,9},{11,10},{13,12},{... | collective-permute-start | bytes 393224 | tf_op jit(solution)/shard_map/ppermute | solution.py:30
  162.8 11.7 %collective-permute-start.33 = (f32[256,2,128]{2,1,0:T(2,128)S(1)}, f32[256,2,128]{2,1,0:T(2,128)S(1)}, u32[]{:S(2)}, u32[]{:S(2)}) collective-permute-start(f32[256,2,128]{2,1,0:T(2,128)S(1)} %constant_dynamic-slice_fusion.12), channel_id=1, source_target_pairs={{0,1},{1,0},{2,3},{3,2},{4,5},{5,4},{6,7},{7,6},{8,9},{9,8},{10,11... | collective-permute-start | bytes 786440 | tf_op jit(solution)/shard_map/ppermute | solution.py:359
  174.7 21.1 %collective-permute-start.34 = (f32[128,2,128]{2,1,0:T(2,128)S(1)}, f32[128,2,128]{2,1,0:T(2,128)S(1)}, u32[]{:S(2)}, u32[]{:S(2)}) collective-permute-start(f32[128,2,128]{2,1,0:T(2,128)S(1)} %constant_dynamic-slice_fusion), channel_id=1, source_target_pairs={{0,2},{1,3},{2,0},{3,1},{4,6},{5,7},{6,4},{7,5},{8,10},{9,11},{10,... | collective-permute-start | bytes 393224 | tf_op jit(solution)/shard_map/ppermute | solution.py:359
  176.8 20.1 %collective-permute-start.28 = (f32[16,2048]{1,0:T(8,128)S(1)}, f32[16,2048]{1,0:T(8,128)S(1)}, u32[]{:S(2)}, u32[]{:S(2)}) collective-permute-start(f32[16,2048]{1,0:T(8,128)S(1)} %constant_dynamic-slice_fusion.2), channel_id=1, source_target_pairs={{0,16},{4,20},{8,24},{12,28},{16,0},{20,4},{24,8},{28,12},{1,17},{... | collective-permute-start | bytes 393224 | tf_op jit(solution)/shard_map/ppermute | solution.py:359
  178.4 20.7 %collective-permute-start.22 = (f32[16,2048]{1,0:T(8,128)S(1)}, f32[16,2048]{1,0:T(8,128)S(1)}, u32[]{:S(2)}, u32[]{:S(2)}) collective-permute-start(f32[16,2048]{1,0:T(8,128)S(1)} %constant_dynamic-slice_fusion.4), channel_id=1, source_target_pairs={{0,8},{4,12},{8,0},{12,4},{16,24},{20,28},{24,16},{28,20},{1,9},{5... | collective-permute-start | bytes 393224 | tf_op jit(solution)/shard_map/ppermute | solution.py:359
  196.1 7.5 %collective-permute-start.35 = (f32[128,2,128]{2,1,0:T(2,128)S(1)}, f32[128,2,128]{2,1,0:T(2,128)S(1)}, u32[]{:S(2)}, u32[]{:S(2)}) collective-permute-start(f32[128,2,128]{2,1,0:T(2,128)S(1)} %multiply_multiply_fusion), channel_id=1, source_target_pairs={{0,2},{1,3},{2,0},{3,1},{4,6},{5,7},{6,4},{7,5},{8,10},{9,11},{10,... | collective-permute-start | bytes 393224 | tf_op jit(solution)/shard_map/ppermute | solution.py:359
  196.9 8.2 %collective-permute-start.29 = (f32[8,2048]{1,0:T(8,128)S(1)}, f32[8,2048]{1,0:T(8,128)S(1)}, u32[]{:S(2)}, u32[]{:S(2)}) collective-permute-start(f32[8,2048]{1,0:T(8,128)S(1)} %constant_dynamic-slice_fusion.1), channel_id=1, source_target_pairs={{0,8},{4,12},{8,0},{12,4},{16,24},{20,28},{24,16},{28,20},{1,9},{5... | collective-permute-start | bytes 196616 | tf_op jit(solution)/shard_map/ppermute | solution.py:359
  199.2 6.1 %collective-permute-start.23 = (f32[8,2048]{1,0:T(8,128)S(1)}, f32[8,2048]{1,0:T(8,128)S(1)}, u32[]{:S(2)}, u32[]{:S(2)}) collective-permute-start(f32[8,2048]{1,0:T(8,128)S(1)} %constant_dynamic-slice_fusion.3), channel_id=1, source_target_pairs={{0,16},{4,20},{8,24},{12,28},{16,0},{20,4},{24,8},{28,12},{1,17},{... | collective-permute-start | bytes 196616 | tf_op jit(solution)/shard_map/ppermute | solution.py:359
  203.7 11.0 %collective-permute-start.36 = (f32[256,2,128]{2,1,0:T(2,128)S(1)}, f32[256,2,128]{2,1,0:T(2,128)S(1)}, u32[]{:S(2)}, u32[]{:S(2)}) collective-permute-start(f32[256,2,128]{2,1,0:T(2,128)S(1)} %pad_maximum_fusion.9), channel_id=1, source_target_pairs={{0,1},{1,0},{2,3},{3,2},{4,5},{5,4},{6,7},{7,6},{8,9},{9,8},{10,11... | collective-permute-start | bytes 786440 | tf_op jit(solution)/shard_map/ppermute | solution.py:359
  205.2 5.1 %collective-permute-start.30 = (f32[8,2048]{1,0:T(8,128)S(1)}, f32[8,2048]{1,0:T(8,128)S(1)}, u32[]{:S(2)}, u32[]{:S(2)}) collective-permute-start(f32[8,2048]{1,0:T(8,128)S(1)} %dynamic-slice_add_fusion.6), channel_id=1, source_target_pairs={{0,8},{4,12},{8,0},{12,4},{16,24},{20,28},{24,16},{28,20},{1,9},{5... | collective-permute-start | bytes 196616 | tf_op jit(solution)/shard_map/ppermute | solution.py:359
  205.3 7.3 %collective-permute-start.24 = (f32[8,2048]{1,0:T(8,128)S(1)}, f32[8,2048]{1,0:T(8,128)S(1)}, u32[]{:S(2)}, u32[]{:S(2)}) collective-permute-start(f32[8,2048]{1,0:T(8,128)S(1)} %dynamic-slice_add_fusion.7), channel_id=1, source_target_pairs={{0,16},{4,20},{8,24},{12,28},{16,0},{20,4},{24,8},{28,12},{1,17},{... | collective-permute-start | bytes 196616 | tf_op jit(solution)/shard_map/ppermute | solution.py:359
  210.4 5.6 %collective-permute-start.31 = (f32[16,2048]{1,0:T(8,128)S(1)}, f32[16,2048]{1,0:T(8,128)S(1)}, u32[]{:S(2)}, u32[]{:S(2)}) collective-permute-start(f32[16,2048]{1,0:T(8,128)S(1)} %pad_maximum_fusion.13), channel_id=1, source_target_pairs={{0,16},{4,20},{8,24},{12,28},{16,0},{20,4},{24,8},{28,12},{1,17},{... | collective-permute-start | bytes 393224 | tf_op jit(solution)/shard_map/ppermute | solution.py:359
  212.7 5.0 %collective-permute-start.25 = (f32[16,2048]{1,0:T(8,128)S(1)}, f32[16,2048]{1,0:T(8,128)S(1)}, u32[]{:S(2)}, u32[]{:S(2)}) collective-permute-start(f32[16,2048]{1,0:T(8,128)S(1)} %pad_maximum_fusion.12), channel_id=1, source_target_pairs={{0,8},{4,12},{8,0},{12,4},{16,24},{20,28},{24,16},{28,20},{1,9},{5... | collective-permute-start | bytes 393224 | tf_op jit(solution)/shard_map/ppermute | solution.py:359
  (12 other events, 113.6 us)

commit v2 on v1

--- a/solution.py
+++ b/solution.py
@@ -19,9 +19,10 @@
 ROOT_HALF = 0.7071067811865476
 
 GROUP = 8
-RING = 32
-CHUNK = 128
+RING = 8
+CHUNK = 320
 PIECE = 512
+DEPTH = 4
 
 
 def shifted(shard, axis, by):
@@ -66,20 +67,27 @@
     cap = chans * slots * blocks_per
     refs = list(refs)
     ent, off = refs[:2]
-    v_ref, tiles_ref, x_ref, u_ref, carry_ref = refs[2:7]
+    v_ref, tiles_ref, x_hbm, u_hbm, carry_ref = refs[2:7]
     refs = refs[7:]
     if not first:
         last_ref, tot_ref, rad_ref = refs[:3]
         refs = refs[3:]
-    adj_ref, hi_ref, lo_ref, cos_ref, sin_ref = refs[:5]
-    img_ref, push_ref, sum_ref, seen_ref, ef_ref, el_ref, pl_ref = refs[5:12]
+    tables, (cos_ref, sin_ref) = refs[:3], refs[3:5]
+    img_hbm, push_hbm, sum_ref, seen_ref, ef_ref, el_ref, pl_ref = refs[5:12]
     big, g_re, g_im, ph_c, ph_s, bacc, ebuf, tbuf, sems = refs[12:21]
+    adj_ref, hi_ref, lo_ref, table_sems = refs[21:25]
+    x_in, u_in, x_out, u_out, in_sems, out_sems = refs[25:31]
     if not first:
-        us, scale = refs[21:23]
+        us, scale = refs[31:33]
     c = pl.program_id(0)
     total = off[chans]
     groups = lax.shift_right_logical(total + (GROUP - 1), GROUP.bit_length() - 1)
-    chunks = lax.shift_right_logical(total + (CHUNK - 1), CHUNK.bit_length() - 1)
+    chunks = sum(
+        (total > begin).astype(jnp.int32) for begin in range(0, cap, CHUNK)
+    )
+    slot = lax.rem(c, DEPTH)
+    x_ref, u_ref = x_in.at[pl.ds(slot, 1)], u_in.at[pl.ds(slot, 1)]
+    img_ref, push_ref = x_out.at[pl.ds(slot, 1)], u_out.at[pl.ds(slot, 1)]
 
     def entry(q):
         where_it_goes, source = split_divide(ent[q], cap)
@@ -106,12 +114,34 @@
         def _(group):
             issue(group)
 
+    def copies_in(channel):
+        place = lax.rem(channel, DEPTH)
+        return (
+            pltpu.make_async_copy(x_hbm.at[channel], x_in.at[place], in_sems.at[0, place]),
+            pltpu.make_async_copy(u_hbm.at[channel], u_in.at[place], in_sems.at[1, place]),
+        )
+
+    def copies_out(channel):
+        place = lax.rem(channel, DEPTH)
+        return (
+            pltpu.make_async_copy(x_out.at[place], img_hbm.at[channel], out_sems.at[0, place]),
+            pltpu.make_async_copy(u_out.at[place], push_hbm.at[channel], out_sems.at[1, place]),
+        )
+
+    def table_copy(k):
+        return pltpu.make_async_copy(tables[k], (adj_ref, hi_ref, lo_ref)[k], table_sems.at[k])
+
     def widen(value):
         return jnp.concatenate([value] * (PIECE // tile), axis=1)
 
     @pl.when(c == 0)
     def _():
         prime()
+        for k in range(3):
+            table_copy(k).start()
+        for channel in range(min(DEPTH, chans)):
+            for copy in copies_in(jnp.int32(channel)):
+                copy.start()
         sum_ref[...] = jnp.zeros_like(sum_ref)
         if not first:
             for band in range(2):
@@ -142,6 +172,8 @@
             def _():
                 issue(group + RING)
 
+        table_copy(0).wait()
+
         @pl.loop(0, chunks)
         def _(chunk):
             at = pl.ds(pl.multiple_of(chunk * CHUNK, CHUNK), CHUNK)
@@ -166,6 +198,14 @@
         _, row, _ = entry(q)
         bacc[pl.ds(row, 1), :] += big[pl.ds(q, 1), :]
 
+    for copy in copies_in(c):
+        copy.wait()
+
+    @pl.when(c >= DEPTH)
+    def _():
+        for copy in copies_out(c - DEPTH):
+            copy.wait()
+
     if not first:
         us[0, 7:8] = carry_ref[pl.ds(c, 1), :]
         for band in range(2):
@@ -213,12 +253,22 @@
         sum_ref[1, r : r + 8] += horizontal * horizontal
         if r == rows - 8:
             pl_ref[pl.ds(c, 1), :] = vertical[7:8]
+    for copy in copies_out(c):
+        copy.start()
+
+    @pl.when(c + DEPTH < chans)
+    def _():
+        for copy in copies_in(c + DEPTH):
+            copy.start()
+
     ef_ref[pl.ds(c, 1), :] = ebuf[0:1]
     el_ref[pl.ds(c, 1), :] = ebuf[rows - 1 : rows]
 
     @pl.when(c == chans - 1)
     def _():
         seen_ref[...] = jnp.zeros_like(seen_ref)
+        table_copy(1).wait()
+        table_copy(2).wait()
 
         @pl.loop(0, chunks)
         def _(chunk):
@@ -259,6 +309,10 @@
             def _():
                 issue(group + RING)
 
+        for channel in range(max(chans - DEPTH, 0), chans):
+            for copy in copies_out(jnp.int32(channel)):
+                copy.wait()
+
 
 def iteration(first, tables, ent, off, v, tiles, x, u, carry, extra=()):
     chans, rows, extent = x.shape
@@ -271,13 +325,8 @@
     def whole(shape):
         return pl.BlockSpec(shape, lambda c, *_: (0,) * len(shape), pipeline_mode=pl.Buffered(1))
 
-    def per_channel(shape):
-        return pl.BlockSpec((1,) + shape, lambda c, *_: (c,) + (0,) * len(shape))
-
-    image_spec, dual_spec = per_channel((rows, extent)), per_channel((2, rows, extent))
-    resident = lambda shape: jax.ShapeDtypeStruct(shape, jnp.float32)
     outs = [x.shape, u.shape, (2, rows, extent), v.shape] + [(chans, extent)] * 3
-    rows_cap = max(cap, CHUNK)
+    rows_cap = pl.cdiv(cap, CHUNK) * CHUNK
     scratch = [
         pltpu.VMEM((rows_cap, extent), jnp.float32),
         pltpu.VMEM((rows_cap, tile), jnp.float32),
@@ -288,27 +337,40 @@
         pltpu.VMEM((rows + 8, extent), jnp.float32),
         pltpu.VMEM((RING * GROUP, tile, tile), jnp.bfloat16),
         pltpu.SemaphoreType.DMA((RING,)),
+        *(pltpu.VMEM(t.shape, t.dtype) for t in tables[:3]),
+        pltpu.SemaphoreType.DMA((3,)),
+        *[pltpu.VMEM((DEPTH, rows, extent), jnp.float32), pltpu.VMEM((DEPTH, 2, rows, extent), jnp.float32)] * 2,
+        *[pltpu.SemaphoreType.DMA((2, DEPTH))] * 2,
     ]
     if not first:
         scratch += [
             pltpu.VMEM((2, rows + 8, extent), jnp.float32),
             pltpu.VMEM((2, rows, extent), jnp.float32),
         ]
+    pin = lambda a: pltpu.with_memory_space_constraint(a, pltpu.HBM)
+    x, u, tiles = pin(x), pin(u), pin(tiles)
+    v = pin(v) if first else v
+    tables = [pin(t) for t in tables]
+    in_hbm = pl.BlockSpec(memory_space=pltpu.HBM)
     operands = [v, tiles, x, u, carry, *extra, *tables]
-    in_specs = [whole(v.shape), pl.BlockSpec(memory_space=pl.ANY), image_spec, dual_spec]
-    in_specs += [whole(a.shape) for a in operands[4:]]
+    in_specs = [whole(v.shape), in_hbm, in_hbm, in_hbm]
+    in_specs += [whole(a.shape) for a in (carry, *extra)] + [in_hbm] * 3
+    in_specs += [whole(a.shape) for a in tables[3:]]
     return pl.pallas_call(
         functools.partial(iteration_kernel, first, dims),
-        out_shape=[resident(s) for s in outs],
+        out_shape=[
+            pltpu.HBM(s, jnp.float32) if k < 2 else jax.ShapeDtypeStruct(s, jnp.float32)
+            for k, s in enumerate(outs)
+        ],
         grid_spec=pltpu.PrefetchScalarGridSpec(
             num_scalar_prefetch=2,
             grid=(chans,),
             in_specs=in_specs,
-            out_specs=[image_spec, dual_spec] + [whole(s) for s in outs[2:]],
+            out_specs=[in_hbm] * 2 + [pl.BlockSpec(s, lambda c, *_, n=len(s): (0,) * n) for s in outs[2:]],
             scratch_shapes=scratch,
         ),
         compiler_params=pltpu.CompilerParams(
-            dimension_semantics=("arbitrary",), vmem_limit_bytes=58 << 20
+            dimension_semantics=("arbitrary",), vmem_limit_bytes=45 << 20
         ),
         name="primal_dual_first" if first else "primal_dual_next",
     )(ent, off, *operands)
@@ -348,7 +410,7 @@
         out_specs=dual_spec,
         scratch_shapes=[pltpu.VMEM((2, rows, extent), jnp.float32)],
         compiler_params=pltpu.CompilerParams(
-            dimension_semantics=("arbitrary",), vmem_limit_bytes=32 << 20
+            dimension_semantics=("arbitrary",), vmem_limit_bytes=8 << 20
         ),
         name="shrink",
     )(push, last, total, radius)
@@ -389,22 +451,27 @@
     return value
 
 
-def chan_orders(count):
-    bits = [1 << k for k in range(count.bit_length() - 1)]
-    inner, outer = bits[:1], bits[1:]
-    half = len(outer) // 2
-    return inner + outer[:half] + outer[half:], inner + outer[half:] + outer[:half]
-
-
 def sum_over_channels(local_sum):
     count = lax.axis_size("chan")
-    if count & (count - 1) or local_sum.shape[1] % count:
+    bands, rows, extent = local_sum.shape
+    if count & (count - 1) or count < 2 or (bands * rows) % count:
         return lax.psum(local_sum, "chan")
-    order_a, order_b = chan_orders(count)
-    vertical, horizontal = local_sum[0], local_sum[1]
-    vertical = double(halve(vertical, "chan", order_a), "chan", order_a)
-    horizontal = double(halve(horizontal, "chan", order_b), "chan", order_b)
-    return jnp.stack([vertical, horizontal])
+    chips = count // 2
+    index = lax.axis_index("chan") // 2
+    value = halve(local_sum.reshape(bands * rows, extent), "chan", [1])
+    value = value.reshape(chips, -1, extent)
+    take = lambda at: lax.dynamic_index_in_dim(value, at, 0, False)
+    parts = [exchange(take(index ^ d), "chan", 2 * d) for d in range(1, chips)]
+    total = sum(parts, take(index))
+    sums = [total] + [exchange(total, "chan", 2 * d) for d in range(1, chips)]
+    placed = []
+    for place in range(chips):
+        chosen = sums[0]
+        for d in range(1, chips):
+            chosen = jnp.where((index ^ place) == d, sums[d], chosen)
+        placed.append(chosen)
+    value = double(jnp.concatenate(placed, axis=0), "chan", [1])
+    return value.reshape(bands, rows, extent)
 
 
 def update_data(seen, data_dual, observed, live):

time: 233 us -> 196 us (0.84); the launches traced: 229 us -> 195 us
  starting transfers between devices: 95.8 us -> 73.5 us
  Pallas kernels: 84 us -> 73.3 us
  waiting for transfers between devices: 20.6 us -> 27.6 us
  other arithmetic: 14.9 us -> 9.77 us
  local copies, waits for them, and re-layouts: 12.3 us -> 9.65 us
    ppermute x32 -> x24, starting transfers between devices: 79.3 us -> 59.1 us  [exchange(): return lax.ppermute(value, axis, [(i, i ^ bit) for i in range(count)])]
    pallas_call x2, Pallas kernels: 74.6 us -> 63.2 us  [iteration(): pl.pallas_call(functools.partial(iteration_kernel, first, dims), out_shap...]
    unnamed x15 -> x3, local copies, waits for them, and re-layouts: 0.72 us -> 5.81 us
    ppermute x32 -> x24, waiting for transfers between devices: 17.1 us -> 21.3 us  [exchange(): return lax.ppermute(value, axis, [(i, i ^ bit) for i in range(count)])]
    ppermute x5, waiting for transfers between devices: 3.57 us -> 6.36 us  [shifted(): return lax.ppermute(shard, axis, pairs)]
    slice x2 -> x0, local copies, waits for them, and re-layouts: 2.58 us -> none  [sum_over_channels(): vertical, horizontal = (local_sum[0], local_sum[1])]
    dynamic_update_slice x2, local copies, waits for them, and re-layouts: 2.98 us -> 0.41 us  [local(): lax.dynamic_update_slice(local_sum, jnp.sum(pushed_last * pushed_last, ax...]
    reduce_sum x2, other arithmetic: 2.51 us -> 0.07 us  [local(): jnp.sum(pushed_last * pushed_last, axis=0)[None, None]]
  transfers between devices with their start and end apart: 37 -> 29, of which waited for: 12 -> 14; matrix products, arithmetic and copies ran while one was open for 11% -> 6% of each run, Pallas kernels for 0% -> 0%
where the time goes in v2:
time: 196 us; the launch traced here: 195 us
  starting transfers between devices  73.5 us (38%)
  Pallas kernels  73.3 us (37%)
  waiting for transfers between devices  27.6 us (14%)
  other arithmetic  9.77 us (5%)
  local copies, waits for them, and re-layouts  9.65 us (5%)
    pallas_call x2, Pallas kernels, iteration(): pl.pallas_call(functools.partial(iteration_kernel, first, dims), out_shap...  63.2 us
    ppermute x24, starting transfers between devices, exchange(): return lax.ppermute(value, axis, [(i, i ^ bit) for i in range(count)])  59.1 us
    ppermute x24, waiting for transfers between devices, exchange(): return lax.ppermute(value, axis, [(i, i ^ bit) for i in range(count)])  21.3 us
    ppermute x5, starting transfers between devices, shifted(): return lax.ppermute(shard, axis, pairs)  14.4 us
    pallas_call x1, Pallas kernels, shrink(): pl.pallas_call(shrink_kernel, out_shape=jax.ShapeDtypeStruct(push.shape,...  10.1 us
    ppermute x5, waiting for transfers between devices, shifted(): return lax.ppermute(shard, axis, pairs)  6.36 us
    unnamed x3, local copies, waits for them, and re-layouts  5.81 us
  transfers between devices with their start and end apart: 29, of which 14 were waited for; matrix products, arithmetic and copies ran while one was open for 6% of the time, Pallas kernels for 0%

profile of v2, /device:TPU:0, one launch (start us, length us, event | category | flops | bytes accessed | tf_op | source)
XLA Modules:
  0.0 195.1 jit_solution(12645719004409037654)
XLA Ops:
  0.6 1.3 slice.26
  2.0 4.9 %collective-permute-start = (f32[16,2048]{1,0:T(8,128)S(1)}, f32[16,2048]{1,0:T(8,128)S(1)}, u32[]{:S(2)}, u32[]{:S(2)}) collective-permute-start(f32[16,2048]{1,0:T(8,128)S(1)} %bitcast.91), channel_id=1, source_target_pairs={{0,1},{1,2},{2,3},{4,5},{5,6},{6,7},{8,9},{9,10},{10,11},{12,13},{... | collective-permute-start | bytes 393224 | tf_op jit(solution)/shard_map/ppermute | solution.py:31
  11.6 30.1 %primal_dual_first.1 = (f32[16,64,2048]{2,1,0:T(8,128)}, f32[16,2,64,2048]{3,2,1,0:T(8,128)}, f32[2,64,2048]{2,1,0:T(8,128)S(1)}, f32[512,2,128]{2,1,0:T(2,128)S...) custom-call(s32[1024]{0:T(1024)S(1)} %select_reduce_fusion.refs_0_, ...), custom_call_target="tpu_custom_call" | custom-call | tf_op jit(solution)/shard_map/primal_dual_first/pallas_call | solution.py:359
  43.2 2.7 %collective-permute-start.1 = (f32[256,2,128]{2,1,0:T(2,128)S(1)}, f32[256,2,128]{2,1,0:T(2,128)S(1)}, u32[]{:S(2)}, u32[]{:S(2)}) collective-permute-start(f32[256,2,128]{2,1,0:T(2,128)S(1)} %constant_dynamic-slice_fusion.5), channel_id=1, source_target_pairs={{0,1},{1,0},{2,3},{3,2},{4,5},{5,4},{6,7},{7,6},{8,9},{9,8},{10,11... | collective-permute-start | bytes 786440 | tf_op jit(solution)/shard_map/ppermute | solution.py:421
  45.9 2.6 %collective-permute-done.6 = f32[16,2048]{1,0:T(8,128)S(1)} collective-permute-done((f32[16,2048]{1,0:T(8,128)S(1)}, f32[16,2048]{1,0:T(8,128)S(1)}, u32[]{:S(2)}, u32[]{:S(2)}) %collective-permute-start.6) | collective-permute-done | bytes 131104 | tf_op jit(solution)/shard_map/ppermute | solution.py:31
  49.1 2.3 %collective-permute-done.1 = f32[256,2,128]{2,1,0:T(2,128)S(1)} collective-permute-done((f32[256,2,128]{2,1,0:T(2,128)S(1)}, f32[256,2,128]{2,1,0:T(2,128)S(1)}, u32[]{:S(2)}, u32[]{:S(2)}) %collective-permute-start.1) | collective-permute-done | bytes 262176 | tf_op jit(solution)/shard_map/ppermute | solution.py:421
  51.5 2.7 %collective-permute-start.2 = (f32[128,2,128]{2,1,0:T(2,128)S(1)}, f32[128,2,128]{2,1,0:T(2,128)S(1)}, u32[]{:S(2)}, u32[]{:S(2)}) collective-permute-start(f32[128,2,128]{2,1,0:T(2,128)S(1)} %constant_dynamic-slice_fusion.4), channel_id=1, source_target_pairs={{0,2},{1,3},{2,0},{3,1},{4,6},{5,7},{6,4},{7,5},{8,10},{9,11},{10,... | collective-permute-start | bytes 393224 | tf_op jit(solution)/shard_map/ppermute | solution.py:421
  54.3 3.7 %collective-permute-start.8 = (f32[16,2048]{1,0:T(8,128)S(1)}, f32[16,2048]{1,0:T(8,128)S(1)}, u32[]{:S(2)}, u32[]{:S(2)}) collective-permute-start(f32[16,2048]{1,0:T(8,128)S(1)} %get-tuple-element.52), channel_id=1, source_target_pairs={{0,8},{4,12},{8,0},{12,4},{16,24},{20,28},{24,16},{28,20},{1,9},{5... | collective-permute-start | bytes 393224 | tf_op jit(solution)/shard_map/ppermute | solution.py:421
  58.0 16.0 %collective-permute-start.10 = (f32[16,2048]{1,0:T(8,128)S(1)}, f32[16,2048]{1,0:T(8,128)S(1)}, u32[]{:S(2)}, u32[]{:S(2)}) collective-permute-start(f32[16,2048]{1,0:T(8,128)S(1)} %get-tuple-element.53), channel_id=1, source_target_pairs={{0,24},{4,28},{8,16},{12,20},{16,8},{20,12},{24,0},{28,4},{1,25},{... | collective-permute-start | bytes 393224 | tf_op jit(solution)/shard_map/ppermute | solution.py:421
  76.7 1.6 collective-permute-done.10
  78.3 1.3 collective-permute-done.9
  79.7 2.1 %collective-permute-start.13 = (f32[16,2048]{1,0:T(8,128)S(1)}, f32[16,2048]{1,0:T(8,128)S(1)}, u32[]{:S(2)}, u32[]{:S(2)}) collective-permute-start(f32[16,2048]{1,0:T(8,128)S(1)} %fusion.6), channel_id=1, source_target_pairs={{0,8},{4,12},{8,0},{12,4},{16,24},{20,28},{24,16},{28,20},{1,9},{5... | collective-permute-start | bytes 393224 | tf_op jit(solution)/shard_map/ppermute | solution.py:421
  81.9 1.4 collective-permute-start.11
  83.6 2.3 %collective-permute-done.13 = f32[16,2048]{1,0:T(8,128)S(1)} collective-permute-done((f32[16,2048]{1,0:T(8,128)S(1)}, f32[16,2048]{1,0:T(8,128)S(1)}, u32[]{:S(2)}, u32[]{:S(2)}) %collective-permute-start.13) | collective-permute-done | bytes 131104 | tf_op jit(solution)/shard_map/ppermute | solution.py:421
  85.9 3.1 %collective-permute-done.12 = f32[16,2048]{1,0:T(8,128)S(1)} collective-permute-done((f32[16,2048]{1,0:T(8,128)S(1)}, f32[16,2048]{1,0:T(8,128)S(1)}, u32[]{:S(2)}, u32[]{:S(2)}) %collective-permute-start.12) | collective-permute-done | bytes 131104 | tf_op jit(solution)/shard_map/ppermute | solution.py:421
  92.1 5.6 %collective-permute-start.15 = (f32[1,2048]{1,0:T(1,128)S(1)}, f32[1,2048]{1,0:T(1,128)S(1)}, u32[]{:S(2)}, u32[]{:S(2)}) collective-permute-start(f32[1,2048]{1,0:T(1,128)S(1)} %slice_bitcast_fusion), channel_id=1, source_target_pairs={{0,1},{1,2},{2,3},{4,5},{5,6},{6,7},{8,9},{9,10},{10,11},{12,13},{... | collective-permute-start | bytes 24584 | tf_op jit(solution)/shard_map/ppermute | solution.py:31
  99.0 33.1 %primal_dual_next.1 = (f32[16,64,2048]{2,1,0:T(8,128)}, f32[16,2,64,2048]{3,2,1,0:T(8,128)}, f32[2,64,2048]{2,1,0:T(8,128)S(1)}, f32[512,2,128]{2,1,0:T(2,128)S(...) custom-call(s32[1024]{0:T(1024)S(1)} %select_reduce_fusion.refs_0_, ...), custom_call_target="tpu_custom_call" | custom-call | tf_op jit(solution)/shard_map/primal_dual_next/pallas_call | solution.py:359
  133.5 3.0 %collective-permute-start.25 = (f32[256,2,128]{2,1,0:T(2,128)S(1)}, f32[256,2,128]{2,1,0:T(2,128)S(1)}, u32[]{:S(2)}, u32[]{:S(2)}) collective-permute-start(f32[256,2,128]{2,1,0:T(2,128)S(1)} %constant_dynamic-slice_fusion.6), channel_id=1, source_target_pairs={{0,1},{1,0},{2,3},{3,2},{4,5},{5,4},{6,7},{7,6},{8,9},{9,8},{10,11... | collective-permute-start | bytes 786440 | tf_op jit(solution)/shard_map/ppermute | solution.py:421
  136.5 2.8 %collective-permute-done.16 = f32[16,2048]{1,0:T(8,128)S(1)} collective-permute-done((f32[16,2048]{1,0:T(8,128)S(1)}, f32[16,2048]{1,0:T(8,128)S(1)}, u32[]{:S(2)}, u32[]{:S(2)}) %collective-permute-start.16) | collective-permute-done | bytes 131104 | tf_op jit(solution)/shard_map/ppermute | solution.py:31
  139.7 2.4 %collective-permute-done.25 = f32[256,2,128]{2,1,0:T(2,128)S(1)} collective-permute-done((f32[256,2,128]{2,1,0:T(2,128)S(1)}, f32[256,2,128]{2,1,0:T(2,128)S(1)}, u32[]{:S(2)}, u32[]{:S(2)}) %collective-permute-start.25) | collective-permute-done | bytes 262176 | tf_op jit(solution)/shard_map/ppermute | solution.py:421
  142.3 2.3 %collective-permute-start.26 = (f32[128,2,128]{2,1,0:T(2,128)S(1)}, f32[128,2,128]{2,1,0:T(2,128)S(1)}, u32[]{:S(2)}, u32[]{:S(2)}) collective-permute-start(f32[128,2,128]{2,1,0:T(2,128)S(1)} %constant_dynamic-slice_fusion), channel_id=1, source_target_pairs={{0,2},{1,3},{2,0},{3,1},{4,6},{5,7},{6,4},{7,5},{8,10},{9,11},{10,... | collective-permute-start | bytes 393224 | tf_op jit(solution)/shard_map/ppermute | solution.py:421
  144.7 1.9 collective-permute-start.18
  146.6 15.0 %collective-permute-start.20 = (f32[16,2048]{1,0:T(8,128)S(1)}, f32[16,2048]{1,0:T(8,128)S(1)}, u32[]{:S(2)}, u32[]{:S(2)}) collective-permute-start(f32[16,2048]{1,0:T(8,128)S(1)} %get-tuple-element.46), channel_id=1, source_target_pairs={{0,24},{4,28},{8,16},{12,20},{16,8},{20,12},{24,0},{28,4},{1,25},{... | collective-permute-start | bytes 393224 | tf_op jit(solution)/shard_map/ppermute | solution.py:421
  162.1 1.3 multiply_multiply_fusion
  163.4 1.9 collective-permute-start.27
  165.9 1.3 collective-permute-done.19
  167.3 2.3 %collective-permute-start.23 = (f32[16,2048]{1,0:T(8,128)S(1)}, f32[16,2048]{1,0:T(8,128)S(1)}, u32[]{:S(2)}, u32[]{:S(2)}) collective-permute-start(f32[16,2048]{1,0:T(8,128)S(1)} %fusion.4), channel_id=1, source_target_pairs={{0,8},{4,12},{8,0},{12,4},{16,24},{20,28},{24,16},{28,20},{1,9},{5... | collective-permute-start | bytes 393224 | tf_op jit(solution)/shard_map/ppermute | solution.py:421
  169.6 1.5 collective-permute-start.21
  172.7 3.4 %collective-permute-done.22 = f32[16,2048]{1,0:T(8,128)S(1)} collective-permute-done((f32[16,2048]{1,0:T(8,128)S(1)}, f32[16,2048]{1,0:T(8,128)S(1)}, u32[]{:S(2)}, u32[]{:S(2)}) %collective-permute-start.22) | collective-permute-done | bytes 131104 | tf_op jit(solution)/shard_map/ppermute | solution.py:421
  176.2 1.5 collective-permute-done.28
  179.2 5.8 %copy-done = f32[16,2,64,2048]{3,2,1,0:T(8,128)S(1)} copy-done((f32[16,2,64,2048]{3,2,1,0:T(8,128)S(1)}, f32[16,2,64,2048]{3,2,1,0:T(8,128)}, u32[]{:S(2)}) %copy-start) | copy-done | bytes 16777240
  185.0 10.1 %shrink.1 = f32[16,2,64,2048]{3,2,1,0:T(8,128)} custom-call(f32[16,2,64,2048]{3,2,1,0:T(8,128)S(1)} %copy-done, f32[16,2048]{1,0:T(8,128)S(1)} %get-tuple-element.30.last_ref, f32[2,64,2048]{2,1,0:T(8,128)S(1)} %bitcast.63, f32[64,1]{1,0:T(8,128)S(1)} %copy.27.refs_9_.rad_ref), custom_call_target="tpu_custom_call" | custom-call | tf_op jit(solution)/shard_map/shrink/pallas_call | solution.py:405
  (91 shorter events, 20.3 us)
Async XLA Ops:
  2.0 9.5 %collective-permute-start = (f32[16,2048]{1,0:T(8,128)S(1)}, f32[16,2048]{1,0:T(8,128)S(1)}, u32[]{:S(2)}, u32[]{:S(2)}) collective-permute-start(f32[16,2048]{1,0:T(8,128)S(1)} %bitcast.91), channel_id=1, source_target_pairs={{0,1},{1,2},{2,3},{4,5},{5,6},{6,7},{8,9},{9,10},{10,11},{12,13},{... | collective-permute-start | bytes 393224 | tf_op jit(solution)/shard_map/ppermute | solution.py:31
  41.7 6.9 %collective-permute-start.6 = (f32[16,2048]{1,0:T(8,128)S(1)}, f32[16,2048]{1,0:T(8,128)S(1)}, u32[]{:S(2)}, u32[]{:S(2)}) collective-permute-start(f32[16,2048]{1,0:T(8,128)S(1)} %get-tuple-element.19), channel_id=1, source_target_pairs={{1,0},{2,1},{3,2},{5,4},{6,5},{7,6},{9,8},{10,9},{11,10},{13,12},{... | collective-permute-start | bytes 393224 | tf_op jit(solution)/shard_map/ppermute | solution.py:31
  43.2 8.1 %collective-permute-start.1 = (f32[256,2,128]{2,1,0:T(2,128)S(1)}, f32[256,2,128]{2,1,0:T(2,128)S(1)}, u32[]{:S(2)}, u32[]{:S(2)}) collective-permute-start(f32[256,2,128]{2,1,0:T(2,128)S(1)} %constant_dynamic-slice_fusion.5), channel_id=1, source_target_pairs={{0,1},{1,0},{2,3},{3,2},{4,5},{5,4},{6,7},{7,6},{8,9},{9,8},{10,11... | collective-permute-start | bytes 786440 | tf_op jit(solution)/shard_map/ppermute | solution.py:421
  48.8 5.3 %collective-permute-start.7 = (f32[64,2048]{1,0:T(8,128)S(1)}, f32[64,2048]{1,0:T(8,128)S(1)}, u32[]{:S(2)}, u32[]{:S(2)}) collective-permute-start(f32[64,2048]{1,0:T(8,128)S(1)} %constant_dynamic-slice_fusion.2), channel_id=1, source_target_pairs={{0,4},{4,0},{8,12},{12,8},{16,20},{20,16},{24,28},{28,24},{1,5},{5... | collective-permute-start | bytes 1572872 | tf_op jit(solution)/shard_map/ppermute | solution.py:421
  51.5 23.0 %collective-permute-start.2 = (f32[128,2,128]{2,1,0:T(2,128)S(1)}, f32[128,2,128]{2,1,0:T(2,128)S(1)}, u32[]{:S(2)}, u32[]{:S(2)}) collective-permute-start(f32[128,2,128]{2,1,0:T(2,128)S(1)} %constant_dynamic-slice_fusion.4), channel_id=1, source_target_pairs={{0,2},{1,3},{2,0},{3,1},{4,6},{5,7},{6,4},{7,5},{8,10},{9,11},{10,... | collective-permute-start | bytes 393224 | tf_op jit(solution)/shard_map/ppermute | solution.py:421
  54.3 22.4 %collective-permute-start.8 = (f32[16,2048]{1,0:T(8,128)S(1)}, f32[16,2048]{1,0:T(8,128)S(1)}, u32[]{:S(2)}, u32[]{:S(2)}) collective-permute-start(f32[16,2048]{1,0:T(8,128)S(1)} %get-tuple-element.52), channel_id=1, source_target_pairs={{0,8},{4,12},{8,0},{12,4},{16,24},{20,28},{24,16},{28,20},{1,9},{5... | collective-permute-start | bytes 393224 | tf_op jit(solution)/shard_map/ppermute | solution.py:421
  58.0 20.3 %collective-permute-start.10 = (f32[16,2048]{1,0:T(8,128)S(1)}, f32[16,2048]{1,0:T(8,128)S(1)}, u32[]{:S(2)}, u32[]{:S(2)}) collective-permute-start(f32[16,2048]{1,0:T(8,128)S(1)} %get-tuple-element.53), channel_id=1, source_target_pairs={{0,24},{4,28},{8,16},{12,20},{16,8},{20,12},{24,0},{28,4},{1,25},{... | collective-permute-start | bytes 393224 | tf_op jit(solution)/shard_map/ppermute | solution.py:421
  74.0 5.7 %collective-permute-start.9 = (f32[16,2048]{1,0:T(8,128)S(1)}, f32[16,2048]{1,0:T(8,128)S(1)}, u32[]{:S(2)}, u32[]{:S(2)}) collective-permute-start(f32[16,2048]{1,0:T(8,128)S(1)} %get-tuple-element.54), channel_id=1, source_target_pairs={{0,16},{4,20},{8,24},{12,28},{16,0},{20,4},{24,8},{28,12},{1,17},{... | collective-permute-start | bytes 393224 | tf_op jit(solution)/shard_map/ppermute | solution.py:421
  75.7 7.7 %collective-permute-start.3 = (f32[128,2,128]{2,1,0:T(2,128)S(1)}, f32[128,2,128]{2,1,0:T(2,128)S(1)}, u32[]{:S(2)}, u32[]{:S(2)}) collective-permute-start(f32[128,2,128]{2,1,0:T(2,128)S(1)} %multiply_multiply_fusion.1), channel_id=1, source_target_pairs={{0,2},{1,3},{2,0},{3,1},{4,6},{5,7},{6,4},{7,5},{8,10},{9,11},{10,... | collective-permute-start | bytes 393224 | tf_op jit(solution)/shard_map/ppermute | solution.py:421
  79.7 6.2 %collective-permute-start.13 = (f32[16,2048]{1,0:T(8,128)S(1)}, f32[16,2048]{1,0:T(8,128)S(1)}, u32[]{:S(2)}, u32[]{:S(2)}) collective-permute-start(f32[16,2048]{1,0:T(8,128)S(1)} %fusion.6), channel_id=1, source_target_pairs={{0,8},{4,12},{8,0},{12,4},{16,24},{20,28},{24,16},{28,20},{1,9},{5... | collective-permute-start | bytes 393224 | tf_op jit(solution)/shard_map/ppermute | solution.py:421
  81.8 7.2 %collective-permute-start.12 = (f32[16,2048]{1,0:T(8,128)S(1)}, f32[16,2048]{1,0:T(8,128)S(1)}, u32[]{:S(2)}, u32[]{:S(2)}) collective-permute-start(f32[16,2048]{1,0:T(8,128)S(1)} %fusion.6), channel_id=1, source_target_pairs={{0,16},{4,20},{8,24},{12,28},{16,0},{20,4},{24,8},{28,12},{1,17},{... | collective-permute-start | bytes 393224 | tf_op jit(solution)/shard_map/ppermute | solution.py:421
  81.9 7.1 %collective-permute-start.11 = (f32[16,2048]{1,0:T(8,128)S(1)}, f32[16,2048]{1,0:T(8,128)S(1)}, u32[]{:S(2)}, u32[]{:S(2)}) collective-permute-start(f32[16,2048]{1,0:T(8,128)S(1)} %fusion.6), channel_id=1, source_target_pairs={{0,24},{4,28},{8,16},{12,20},{16,8},{20,12},{24,0},{28,4},{1,25},{... | collective-permute-start | bytes 393224 | tf_op jit(solution)/shard_map/ppermute | solution.py:421
  83.5 7.2 %collective-permute-start.4 = (f32[256,2,128]{2,1,0:T(2,128)S(1)}, f32[256,2,128]{2,1,0:T(2,128)}, u32[]{:S(2)}, u32[]{:S(2)}) collective-permute-start(f32[256,2,128]{2,1,0:T(2,128)S(1)} %pad_maximum_fusion.6), channel_id=1, source_target_pairs={{0,1},{1,0},{2,3},{3,2},{4,5},{5,4},{6,7},{7,6},{8,9},{9,8},{10,11... | collective-permute-start | bytes 786440 | tf_op jit(solution)/shard_map/ppermute | solution.py:421
  89.1 2.8 %collective-permute-start.14 = (f32[64,2048]{1,0:T(8,128)S(1)}, f32[64,2048]{1,0:T(8,128)S(1)}, u32[]{:S(2)}, u32[]{:S(2)}) collective-permute-start(f32[64,2048]{1,0:T(8,128)S(1)} %pad_maximum_fusion.3), channel_id=1, source_target_pairs={{0,4},{4,0},{8,12},{12,8},{16,20},{20,16},{24,28},{28,24},{1,5},{5... | collective-permute-start | bytes 1572872 | tf_op jit(solution)/shard_map/ppermute | solution.py:421
  89.4 9.5 %collective-permute-start.5 = (f32[16,2048]{1,0:T(8,128)S(1)}, f32[16,2048]{1,0:T(8,128)S(1)}, u32[]{:S(2)}, u32[]{:S(2)}) collective-permute-start(f32[16,2048]{1,0:T(8,128)S(1)} %get-tuple-element.20), channel_id=1, source_target_pairs={{0,1},{1,2},{2,3},{4,5},{5,6},{6,7},{8,9},{9,10},{10,11},{12,13},{... | collective-permute-start | bytes 393224 | tf_op jit(solution)/shard_map/ppermute | solution.py:31
  92.1 6.7 %collective-permute-start.15 = (f32[1,2048]{1,0:T(1,128)S(1)}, f32[1,2048]{1,0:T(1,128)S(1)}, u32[]{:S(2)}, u32[]{:S(2)}) collective-permute-start(f32[1,2048]{1,0:T(1,128)S(1)} %slice_bitcast_fusion), channel_id=1, source_target_pairs={{0,1},{1,2},{2,3},{4,5},{5,6},{6,7},{8,9},{9,10},{10,11},{12,13},{... | collective-permute-start | bytes 24584 | tf_op jit(solution)/shard_map/ppermute | solution.py:31
  132.1 7.2 %collective-permute-start.16 = (f32[16,2048]{1,0:T(8,128)S(1)}, f32[16,2048]{1,0:T(8,128)S(1)}, u32[]{:S(2)}, u32[]{:S(2)}) collective-permute-start(f32[16,2048]{1,0:T(8,128)S(1)} %get-tuple-element.26), channel_id=1, source_target_pairs={{1,0},{2,1},{3,2},{5,4},{6,5},{7,6},{9,8},{10,9},{11,10},{13,12},{... | collective-permute-start | bytes 393224 | tf_op jit(solution)/shard_map/ppermute | solution.py:31
  133.5 8.6 %collective-permute-start.25 = (f32[256,2,128]{2,1,0:T(2,128)S(1)}, f32[256,2,128]{2,1,0:T(2,128)S(1)}, u32[]{:S(2)}, u32[]{:S(2)}) collective-permute-start(f32[256,2,128]{2,1,0:T(2,128)S(1)} %constant_dynamic-slice_fusion.6), channel_id=1, source_target_pairs={{0,1},{1,0},{2,3},{3,2},{4,5},{5,4},{6,7},{7,6},{8,9},{9,8},{10,11... | collective-permute-start | bytes 786440 | tf_op jit(solution)/shard_map/ppermute | solution.py:421
  139.6 4.9 %collective-permute-start.17 = (f32[64,2048]{1,0:T(8,128)S(1)}, f32[64,2048]{1,0:T(8,128)S(1)}, u32[]{:S(2)}, u32[]{:S(2)}) collective-permute-start(f32[64,2048]{1,0:T(8,128)S(1)} %constant_dynamic-slice_fusion.1), channel_id=1, source_target_pairs={{0,4},{4,0},{8,12},{12,8},{16,20},{20,16},{24,28},{28,24},{1,5},{5... | collective-permute-start | bytes 1572872 | tf_op jit(solution)/shard_map/ppermute | solution.py:421
  142.3 19.8 %collective-permute-start.26 = (f32[128,2,128]{2,1,0:T(2,128)S(1)}, f32[128,2,128]{2,1,0:T(2,128)S(1)}, u32[]{:S(2)}, u32[]{:S(2)}) collective-permute-start(f32[128,2,128]{2,1,0:T(2,128)S(1)} %constant_dynamic-slice_fusion), channel_id=1, source_target_pairs={{0,2},{1,3},{2,0},{3,1},{4,6},{5,7},{6,4},{7,5},{8,10},{9,11},{10,... | collective-permute-start | bytes 393224 | tf_op jit(solution)/shard_map/ppermute | solution.py:421
  144.7 20.6 %collective-permute-start.18 = (f32[16,2048]{1,0:T(8,128)S(1)}, f32[16,2048]{1,0:T(8,128)S(1)}, u32[]{:S(2)}, u32[]{:S(2)}) collective-permute-start(f32[16,2048]{1,0:T(8,128)S(1)} %get-tuple-element.45), channel_id=1, source_target_pairs={{0,8},{4,12},{8,0},{12,4},{16,24},{20,28},{24,16},{28,20},{1,9},{5... | collective-permute-start | bytes 393224 | tf_op jit(solution)/shard_map/ppermute | solution.py:421
  146.6 19.4 %collective-permute-start.20 = (f32[16,2048]{1,0:T(8,128)S(1)}, f32[16,2048]{1,0:T(8,128)S(1)}, u32[]{:S(2)}, u32[]{:S(2)}) collective-permute-start(f32[16,2048]{1,0:T(8,128)S(1)} %get-tuple-element.46), channel_id=1, source_target_pairs={{0,24},{4,28},{8,16},{12,20},{16,8},{20,12},{24,0},{28,4},{1,25},{... | collective-permute-start | bytes 393224 | tf_op jit(solution)/shard_map/ppermute | solution.py:421
  161.6 5.7 %collective-permute-start.19 = (f32[16,2048]{1,0:T(8,128)S(1)}, f32[16,2048]{1,0:T(8,128)S(1)}, u32[]{:S(2)}, u32[]{:S(2)}) collective-permute-start(f32[16,2048]{1,0:T(8,128)S(1)} %get-tuple-element.47), channel_id=1, source_target_pairs={{0,16},{4,20},{8,24},{12,28},{16,0},{20,4},{24,8},{28,12},{1,17},{... | collective-permute-start | bytes 393224 | tf_op jit(solution)/shard_map/ppermute | solution.py:421
  163.4 7.8 %collective-permute-start.27 = (f32[128,2,128]{2,1,0:T(2,128)S(1)}, f32[128,2,128]{2,1,0:T(2,128)S(1)}, u32[]{:S(2)}, u32[]{:S(2)}) collective-permute-start(f32[128,2,128]{2,1,0:T(2,128)S(1)} %multiply_multiply_fusion), channel_id=1, source_target_pairs={{0,2},{1,3},{2,0},{3,1},{4,6},{5,7},{6,4},{7,5},{8,10},{9,11},{10,... | collective-permute-start | bytes 393224 | tf_op jit(solution)/shard_map/ppermute | solution.py:421
  167.3 5.3 %collective-permute-start.23 = (f32[16,2048]{1,0:T(8,128)S(1)}, f32[16,2048]{1,0:T(8,128)S(1)}, u32[]{:S(2)}, u32[]{:S(2)}) collective-permute-start(f32[16,2048]{1,0:T(8,128)S(1)} %fusion.4), channel_id=1, source_target_pairs={{0,8},{4,12},{8,0},{12,4},{16,24},{20,28},{24,16},{28,20},{1,9},{5... | collective-permute-start | bytes 393224 | tf_op jit(solution)/shard_map/ppermute | solution.py:421
  169.6 6.4 %collective-permute-start.22 = (f32[16,2048]{1,0:T(8,128)S(1)}, f32[16,2048]{1,0:T(8,128)S(1)}, u32[]{:S(2)}, u32[]{:S(2)}) collective-permute-start(f32[16,2048]{1,0:T(8,128)S(1)} %fusion.4), channel_id=1, source_target_pairs={{0,16},{4,20},{8,24},{12,28},{16,0},{20,4},{24,8},{28,12},{1,17},{... | collective-permute-start | bytes 393224 | tf_op jit(solution)/shard_map/ppermute | solution.py:421
  169.6 6.4 %collective-permute-start.21 = (f32[16,2048]{1,0:T(8,128)S(1)}, f32[16,2048]{1,0:T(8,128)S(1)}, u32[]{:S(2)}, u32[]{:S(2)}) collective-permute-start(f32[16,2048]{1,0:T(8,128)S(1)} %fusion.4), channel_id=1, source_target_pairs={{0,24},{4,28},{8,16},{12,20},{16,8},{20,12},{24,0},{28,4},{1,25},{... | collective-permute-start | bytes 393224 | tf_op jit(solution)/shard_map/ppermute | solution.py:421
  171.3 6.4 %collective-permute-start.28 = (f32[256,2,128]{2,1,0:T(2,128)S(1)}, f32[256,2,128]{2,1,0:T(2,128)S(1)}, u32[]{:S(2)}, u32[]{:S(2)}) collective-permute-start(f32[256,2,128]{2,1,0:T(2,128)S(1)} %pad_maximum_fusion.7), channel_id=1, source_target_pairs={{0,1},{1,0},{2,3},{3,2},{4,5},{5,4},{6,7},{7,6},{8,9},{9,8},{10,11... | collective-permute-start | bytes 786440 | tf_op jit(solution)/shard_map/ppermute | solution.py:421
  176.2 2.8 %collective-permute-start.24 = (f32[64,2048]{1,0:T(8,128)S(1)}, f32[64,2048]{1,0:T(8,128)S(1)}, u32[]{:S(2)}, u32[]{:S(2)}) collective-permute-start(f32[64,2048]{1,0:T(8,128)S(1)} %pad_maximum_fusion.4), channel_id=1, source_target_pairs={{0,4},{4,0},{8,12},{12,8},{16,20},{20,16},{24,28},{28,24},{1,5},{5... | collective-permute-start | bytes 1572872 | tf_op jit(solution)/shard_map/ppermute | solution.py:421
  179.2 5.8 %copy-start = (f32[16,2,64,2048]{3,2,1,0:T(8,128)S(1)}, f32[16,2,64,2048]{3,2,1,0:T(8,128)}, u32[]{:S(2)}) copy-start(f32[16,2,64,2048]{3,2,1,0:T(8,128)} %get-tuple-element.24.push_ref) | copy-start | bytes 50331652

commit v3 on v2

--- a/solution.py
+++ b/solution.py
@@ -19,10 +19,10 @@
 ROOT_HALF = 0.7071067811865476
 
 GROUP = 8
-RING = 8
-CHUNK = 320
+RING = 36
+CHUNK = 352
 PIECE = 512
-DEPTH = 4
+DEPTH = 3
 
 
 def shifted(shard, axis, by):
@@ -188,7 +188,7 @@
                 )
                 big[at, j : j + PIECE] = turn_c * even - turn_s * odd
 
-        prime()
+        pl.when(groups > RING)(prime)
 
     start, end = off[c], off[c + 1]
     bacc[...] = jnp.zeros_like(bacc)
@@ -247,8 +247,15 @@
         right = jnp.where(column == extent - 1, 0.0, pltpu.roll(here, extent - 1, 1))
         vertical = dual(0, r) + (STEP_PRIOR * ROOT_HALF) * (below - here)
         horizontal = dual(1, r) + (STEP_PRIOR * ROOT_HALF) * (right - here)
-        push_ref[0, 0, r : r + 8] = vertical
-        push_ref[0, 1, r : r + 8] = horizontal
+        if push_ref.dtype == jnp.float32:
+            push_ref[0, 0, r : r + 8] = vertical
+            push_ref[0, 1, r : r + 8] = horizontal
+        elif r % 16 == 0:
+            upper = vertical, horizontal
+        else:
+            for band, value in enumerate((vertical, horizontal)):
+                pair = jnp.concatenate([upper[band], value], axis=0)
+                push_ref[0, band, r - 8 : r + 8] = pair.astype(push_ref.dtype)
         sum_ref[0, r : r + 8] += vertical * vertical
         sum_ref[1, r : r + 8] += horizontal * horizontal
         if r == rows - 8:
@@ -292,7 +299,12 @@
 
         @pl.loop(0, groups)
         def _(group):
-            base = await_group(group)
+            base = lax.rem(group, RING) * GROUP
+
+            @pl.when(groups > RING)
+            def _():
+                await_group(group)
+
             at = pl.ds(pl.multiple_of(group * GROUP, GROUP), GROUP)
             lhs = jnp.concatenate([g_re[at, :], g_im[at, :]], axis=0).astype(jnp.bfloat16)
             for t in range(GROUP):
@@ -314,7 +326,7 @@
                 copy.wait()
 
 
-def iteration(first, tables, ent, off, v, tiles, x, u, carry, extra=()):
+def iteration(first, final, tables, ent, off, v, tiles, x, u, carry, extra=()):
     chans, rows, extent = x.shape
     tile = tiles.shape[-1]
     slots = v.shape[0] // chans
@@ -326,6 +338,7 @@
         return pl.BlockSpec(shape, lambda c, *_: (0,) * len(shape), pipeline_mode=pl.Buffered(1))
 
     outs = [x.shape, u.shape, (2, rows, extent), v.shape] + [(chans, extent)] * 3
+    push_type = jnp.bfloat16 if final and rows % 16 == 0 else jnp.float32
     rows_cap = pl.cdiv(cap, CHUNK) * CHUNK
     scratch = [
         pltpu.VMEM((rows_cap, extent), jnp.float32),
@@ -339,7 +352,10 @@
         pltpu.SemaphoreType.DMA((RING,)),
         *(pltpu.VMEM(t.shape, t.dtype) for t in tables[:3]),
         pltpu.SemaphoreType.DMA((3,)),
-        *[pltpu.VMEM((DEPTH, rows, extent), jnp.float32), pltpu.VMEM((DEPTH, 2, rows, extent), jnp.float32)] * 2,
+        pltpu.VMEM((DEPTH, rows, extent), jnp.float32),
+        pltpu.VMEM((DEPTH, 2, rows, extent), jnp.float32),
+        pltpu.VMEM((DEPTH, rows, extent), jnp.float32),
+        pltpu.VMEM((DEPTH, 2, rows, extent), push_type),
         *[pltpu.SemaphoreType.DMA((2, DEPTH))] * 2,
     ]
     if not first:
@@ -359,7 +375,7 @@
     return pl.pallas_call(
         functools.partial(iteration_kernel, first, dims),
         out_shape=[
-            pltpu.HBM(s, jnp.float32) if k < 2 else jax.ShapeDtypeStruct(s, jnp.float32)
+            pltpu.HBM(s, push_type if k == 1 else jnp.float32) if k < 2 else jax.ShapeDtypeStruct(s, jnp.float32)
             for k, s in enumerate(outs)
         ],
         grid_spec=pltpu.PrefetchScalarGridSpec(
@@ -370,7 +386,7 @@
             scratch_shapes=scratch,
         ),
         compiler_params=pltpu.CompilerParams(
-            dimension_semantics=("arbitrary",), vmem_limit_bytes=45 << 20
+            dimension_semantics=("arbitrary",), vmem_limit_bytes=46 << 20
         ),
         name="primal_dual_first" if first else "primal_dual_next",
     )(ent, off, *operands)
@@ -387,12 +403,13 @@
                 norms = jnp.sqrt(tot_ref[band, r : r + 8] + 1e-06)
                 scale[band, r : r + 8] = jnp.minimum(1.0, rad_ref[r : r + 8] / norms)
 
+    strip = 16 if rows % 16 == 0 else 8
     for band in range(2):
-        for r in range(0, rows, 8):
-            value = push_ref[0, band, r : r + 8]
-            if band == 0 and r == rows - 8:
-                value = jnp.concatenate([value[:7], last_ref[pl.ds(c, 1), :]], axis=0)
-            out_ref[0, band, r : r + 8] = value * scale[band, r : r + 8]
+        for r in range(0, rows, strip):
+            value = push_ref[0, band, r : r + strip].astype(jnp.float32)
+            if band == 0 and r == rows - strip:
+                value = jnp.concatenate([value[:-1], last_ref[pl.ds(c, 1), :]], axis=0)
+            out_ref[0, band, r : r + strip] = value * scale[band, r : r + strip]
 
 
 def shrink(push, last, total, radius):
@@ -527,7 +544,7 @@
     extra = ()
     for rounds in range(ITERS):
         image, dual, local_sum, seen, first_row, last_row, pushed_last = iteration(
-            rounds == 0, tables, ent, off, data_dual, tiles, image, dual, carry, extra
+            rounds == 0, rounds == ITERS - 1, tables, ent, off, data_dual, tiles, image, dual, carry, extra
         )
         half_step = STEP_PRIOR * ROOT_HALF
         pushed_last = pushed_last + half_step * shifted(first_row, "facet", -1)

time: 196 us -> 185 us (0.944)
  starting transfers between devices: 73.5 us -> 67.4 us
  local copies, waits for them, and re-layouts: 9.65 us -> 3.89 us
  waiting for transfers between devices: 27.6 us -> 32.9 us
  Pallas kernels: 73.3 us -> 68.5 us
    ppermute x24, starting transfers between devices: 59.1 us -> 52.8 us  [exchange(): return lax.ppermute(value, axis, [(i, i ^ bit) for i in range(count)])]
    unnamed x3 -> x5, local copies, waits for them, and re-layouts: 5.81 us -> 0.05 us
    pallas_call x2, Pallas kernels: 63.2 us -> 59 us  [iteration(): pl.pallas_call(functools.partial(iteration_kernel, first, dims), out_shap...]
    ppermute x5, waiting for transfers between devices: 6.36 us -> 9.29 us  [shifted(): return lax.ppermute(shard, axis, pairs)]
    ppermute x24, waiting for transfers between devices: 21.3 us -> 23.6 us  [exchange(): return lax.ppermute(value, axis, [(i, i ^ bit) for i in range(count)])]
  transfers between devices with their start and end apart: 29 -> 29, of which waited for: 14 -> 14; matrix products, arithmetic and copies ran while one was open for 6% -> 7% of each run, Pallas kernels for 0% -> 0%
where the time goes in v3:
time: 185 us; the launch traced here: 184 us
  Pallas kernels  68.5 us (37%)
  starting transfers between devices  67.4 us (36%)
  waiting for transfers between devices  32.9 us (18%)
  other arithmetic  9.77 us (5%)
  local copies, waits for them, and re-layouts  3.89 us (2%)
    pallas_call x2, Pallas kernels, iteration(): pl.pallas_call(functools.partial(iteration_kernel, first, dims), out_shap...  59 us
    ppermute x24, starting transfers between devices, exchange(): return lax.ppermute(value, axis, [(i, i ^ bit) for i in range(count)])  52.8 us
    ppermute x24, waiting for transfers between devices, exchange(): return lax.ppermute(value, axis, [(i, i ^ bit) for i in range(count)])  23.6 us
    ppermute x5, starting transfers between devices, shifted(): return lax.ppermute(shard, axis, pairs)  14.6 us
    pallas_call x1, Pallas kernels, shrink(): pl.pallas_call(shrink_kernel, out_shape=jax.ShapeDtypeStruct(push.shape,...  9.53 us
    ppermute x5, waiting for transfers between devices, shifted(): return lax.ppermute(shard, axis, pairs)  9.29 us
  transfers between devices with their start and end apart: 29, of which 14 were waited for; matrix products, arithmetic and copies ran while one was open for 7% of the time, Pallas kernels for 0%

profile of v3, /device:TPU:0, one launch (start us, length us, event | category | flops | bytes accessed | tf_op | source)
XLA Modules:
  0.0 183.8 jit_solution(10814419901872267740)
XLA Ops:
  0.6 1.3 slice.26
  2.0 4.9 %collective-permute-start = (f32[16,2048]{1,0:T(8,128)S(1)}, f32[16,2048]{1,0:T(8,128)S(1)}, u32[]{:S(2)}, u32[]{:S(2)}) collective-permute-start(f32[16,2048]{1,0:T(8,128)S(1)} %bitcast.93), channel_id=1, source_target_pairs={{0,1},{1,2},{2,3},{4,5},{5,6},{6,7},{8,9},{9,10},{10,11},{12,13},{... | collective-permute-start | bytes 393224 | tf_op jit(solution)/shard_map/ppermute | solution.py:31
  11.6 27.9 %primal_dual_first.1 = (f32[16,64,2048]{2,1,0:T(8,128)}, f32[16,2,64,2048]{3,2,1,0:T(8,128)}, f32[2,64,2048]{2,1,0:T(8,128)S(1)}, f32[512,2,128]{2,1,0:T(2,128)S...) custom-call(s32[1024]{0:T(1024)S(1)} %select_reduce_fusion.refs_0_, ...), custom_call_target="tpu_custom_call" | custom-call | tf_op jit(solution)/shard_map/primal_dual_first/pallas_call | solution.py:375
  39.5 1.3 collective-permute-start.6
  41.0 2.7 %collective-permute-start.1 = (f32[256,2,128]{2,1,0:T(2,128)S(1)}, f32[256,2,128]{2,1,0:T(2,128)S(1)}, u32[]{:S(2)}, u32[]{:S(2)}) collective-permute-start(f32[256,2,128]{2,1,0:T(2,128)S(1)} %constant_dynamic-slice_fusion.5), channel_id=1, source_target_pairs={{0,1},{1,0},{2,3},{3,2},{4,5},{5,4},{6,7},{7,6},{8,9},{9,8},{10,11... | collective-permute-start | bytes 786440 | tf_op jit(solution)/shard_map/ppermute | solution.py:438
  43.7 4.1 %collective-permute-done.6 = f32[16,2048]{1,0:T(8,128)S(1)} collective-permute-done((f32[16,2048]{1,0:T(8,128)S(1)}, f32[16,2048]{1,0:T(8,128)S(1)}, u32[]{:S(2)}, u32[]{:S(2)}) %collective-permute-start.6) | collective-permute-done | bytes 131104 | tf_op jit(solution)/shard_map/ppermute | solution.py:31
  48.3 3.0 %collective-permute-done.1 = f32[256,2,128]{2,1,0:T(2,128)S(1)} collective-permute-done((f32[256,2,128]{2,1,0:T(2,128)S(1)}, f32[256,2,128]{2,1,0:T(2,128)S(1)}, u32[]{:S(2)}, u32[]{:S(2)}) %collective-permute-start.1) | collective-permute-done | bytes 262176 | tf_op jit(solution)/shard_map/ppermute | solution.py:438
  51.5 3.4 %collective-permute-start.2 = (f32[128,2,128]{2,1,0:T(2,128)S(1)}, f32[128,2,128]{2,1,0:T(2,128)S(1)}, u32[]{:S(2)}, u32[]{:S(2)}) collective-permute-start(f32[128,2,128]{2,1,0:T(2,128)S(1)} %constant_dynamic-slice_fusion.4), channel_id=1, source_target_pairs={{0,2},{1,3},{2,0},{3,1},{4,6},{5,7},{6,4},{7,5},{8,10},{9,11},{10,... | collective-permute-start | bytes 393224 | tf_op jit(solution)/shard_map/ppermute | solution.py:438
  55.5 15.0 %collective-permute-start.10 = (f32[16,2048]{1,0:T(8,128)S(1)}, f32[16,2048]{1,0:T(8,128)S(1)}, u32[]{:S(2)}, u32[]{:S(2)}) collective-permute-start(f32[16,2048]{1,0:T(8,128)S(1)} %get-tuple-element.53), channel_id=1, source_target_pairs={{0,24},{4,28},{8,16},{12,20},{16,8},{20,12},{24,0},{28,4},{1,25},{... | collective-permute-start | bytes 393224 | tf_op jit(solution)/shard_map/ppermute | solution.py:438
  73.1 2.0 %collective-permute-done.10 = f32[16,2048]{1,0:T(8,128)S(1)} collective-permute-done((f32[16,2048]{1,0:T(8,128)S(1)}, f32[16,2048]{1,0:T(8,128)S(1)}, u32[]{:S(2)}, u32[]{:S(2)}) %collective-permute-start.10) | collective-permute-done | bytes 131104 | tf_op jit(solution)/shard_map/ppermute | solution.py:438
  75.1 1.3 collective-permute-done.9
  76.4 1.8 collective-permute-start.13
  78.5 1.5 collective-permute-start.11
  80.2 2.5 %collective-permute-done.13 = f32[16,2048]{1,0:T(8,128)S(1)} collective-permute-done((f32[16,2048]{1,0:T(8,128)S(1)}, f32[16,2048]{1,0:T(8,128)S(1)}, u32[]{:S(2)}, u32[]{:S(2)}) %collective-permute-start.13) | collective-permute-done | bytes 131104 | tf_op jit(solution)/shard_map/ppermute | solution.py:438
  82.7 3.1 %collective-permute-done.12 = f32[16,2048]{1,0:T(8,128)S(1)} collective-permute-done((f32[16,2048]{1,0:T(8,128)S(1)}, f32[16,2048]{1,0:T(8,128)S(1)}, u32[]{:S(2)}, u32[]{:S(2)}) %collective-permute-start.12) | collective-permute-done | bytes 131104 | tf_op jit(solution)/shard_map/ppermute | solution.py:438
  86.2 1.6 collective-permute-start.5
  89.3 5.5 %collective-permute-start.15 = (f32[1,2048]{1,0:T(1,128)S(1)}, f32[1,2048]{1,0:T(1,128)S(1)}, u32[]{:S(2)}, u32[]{:S(2)}) collective-permute-start(f32[1,2048]{1,0:T(1,128)S(1)} %slice_bitcast_fusion), channel_id=1, source_target_pairs={{0,1},{1,2},{2,3},{4,5},{5,6},{6,7},{8,9},{9,10},{10,11},{12,13},{... | collective-permute-start | bytes 24584 | tf_op jit(solution)/shard_map/ppermute | solution.py:31
  96.1 31.1 %primal_dual_next.1 = (f32[16,64,2048]{2,1,0:T(8,128)}, bf16[16,2,64,2048]{3,2,1,0:T(8,128)(2,1)}, f32[2,64,2048]{2,1,0:T(8,128)S(1)}, f32[512,2,128]{2,1,0:T(2,...) custom-call(s32[1024]{0:T(1024)S(1)} %select_reduce_fusion.refs_0_, ...), custom_call_target="tpu_custom_call" | custom-call | tf_op jit(solution)/shard_map/primal_dual_next/pallas_call | solution.py:375
  127.2 1.3 collective-permute-start.16
  128.5 2.7 %collective-permute-start.25 = (f32[256,2,128]{2,1,0:T(2,128)S(1)}, f32[256,2,128]{2,1,0:T(2,128)S(1)}, u32[]{:S(2)}, u32[]{:S(2)}) collective-permute-start(f32[256,2,128]{2,1,0:T(2,128)S(1)} %constant_dynamic-slice_fusion.6), channel_id=1, source_target_pairs={{0,1},{1,0},{2,3},{3,2},{4,5},{5,4},{6,7},{7,6},{8,9},{9,8},{10,11... | collective-permute-start | bytes 786440 | tf_op jit(solution)/shard_map/ppermute | solution.py:438
  131.3 4.3 %collective-permute-done.16 = f32[16,2048]{1,0:T(8,128)S(1)} collective-permute-done((f32[16,2048]{1,0:T(8,128)S(1)}, f32[16,2048]{1,0:T(8,128)S(1)}, u32[]{:S(2)}, u32[]{:S(2)}) %collective-permute-start.16) | collective-permute-done | bytes 131104 | tf_op jit(solution)/shard_map/ppermute | solution.py:31
  135.9 3.3 %collective-permute-done.25 = f32[256,2,128]{2,1,0:T(2,128)S(1)} collective-permute-done((f32[256,2,128]{2,1,0:T(2,128)S(1)}, f32[256,2,128]{2,1,0:T(2,128)S(1)}, u32[]{:S(2)}, u32[]{:S(2)}) %collective-permute-start.25) | collective-permute-done | bytes 262176 | tf_op jit(solution)/shard_map/ppermute | solution.py:438
  139.4 1.8 collective-permute-start.26
  141.4 15.4 %collective-permute-start.20 = (f32[16,2048]{1,0:T(8,128)S(1)}, f32[16,2048]{1,0:T(8,128)S(1)}, u32[]{:S(2)}, u32[]{:S(2)}) collective-permute-start(f32[16,2048]{1,0:T(8,128)S(1)} %get-tuple-element.46), channel_id=1, source_target_pairs={{0,24},{4,28},{8,16},{12,20},{16,8},{20,12},{24,0},{28,4},{1,25},{... | collective-permute-start | bytes 393224 | tf_op jit(solution)/shard_map/ppermute | solution.py:438
  157.3 1.3 multiply_multiply_fusion
  158.6 1.4 collective-permute-start.27
  161.2 1.3 collective-permute-done.19
  162.6 2.1 %collective-permute-start.23 = (f32[16,2048]{1,0:T(8,128)S(1)}, f32[16,2048]{1,0:T(8,128)S(1)}, u32[]{:S(2)}, u32[]{:S(2)}) collective-permute-start(f32[16,2048]{1,0:T(8,128)S(1)} %fusion.4), channel_id=1, source_target_pairs={{0,8},{4,12},{8,0},{12,4},{16,24},{20,28},{24,16},{28,20},{1,9},{5... | collective-permute-start | bytes 393224 | tf_op jit(solution)/shard_map/ppermute | solution.py:438
  164.8 1.4 collective-permute-start.21
  166.7 1.5 collective-permute-done.23
  168.2 3.3 %collective-permute-done.22 = f32[16,2048]{1,0:T(8,128)S(1)} collective-permute-done((f32[16,2048]{1,0:T(8,128)S(1)}, f32[16,2048]{1,0:T(8,128)S(1)}, u32[]{:S(2)}, u32[]{:S(2)}) %collective-permute-start.22) | collective-permute-done | bytes 131104 | tf_op jit(solution)/shard_map/ppermute | solution.py:438
  174.2 9.5 %shrink.1 = f32[16,2,64,2048]{3,2,1,0:T(8,128)} custom-call(bf16[16,2,64,2048]{3,2,1,0:T(8,128)(2,1)S(1)} %bitcast.62, f32[16,2048]{1,0:T(8,128)S(1)} %get-tuple-element.30.last_ref, f32[2,64,2048]{2,1,0:T(8,128)S(1)} %bitcast.65, f32[64,1]{1,0:T(8,128)S(1)} %copy.27.refs_9_.rad_ref), custom_call_target="tpu_custom_call" | custom-call | tf_op jit(solution)/shard_map/shrink/pallas_call | solution.py:422
  (94 shorter events, 17.9 us)
Async XLA Ops:
  2.0 9.5 %collective-permute-start = (f32[16,2048]{1,0:T(8,128)S(1)}, f32[16,2048]{1,0:T(8,128)S(1)}, u32[]{:S(2)}, u32[]{:S(2)}) collective-permute-start(f32[16,2048]{1,0:T(8,128)S(1)} %bitcast.93), channel_id=1, source_target_pairs={{0,1},{1,2},{2,3},{4,5},{5,6},{6,7},{8,9},{9,10},{10,11},{12,13},{... | collective-permute-start | bytes 393224 | tf_op jit(solution)/shard_map/ppermute | solution.py:31
  39.5 8.3 %collective-permute-start.6 = (f32[16,2048]{1,0:T(8,128)S(1)}, f32[16,2048]{1,0:T(8,128)S(1)}, u32[]{:S(2)}, u32[]{:S(2)}) collective-permute-start(f32[16,2048]{1,0:T(8,128)S(1)} %get-tuple-element.19), channel_id=1, source_target_pairs={{1,0},{2,1},{3,2},{5,4},{6,5},{7,6},{9,8},{10,9},{11,10},{13,12},{... | collective-permute-start | bytes 393224 | tf_op jit(solution)/shard_map/ppermute | solution.py:31
  41.0 10.3 %collective-permute-start.1 = (f32[256,2,128]{2,1,0:T(2,128)S(1)}, f32[256,2,128]{2,1,0:T(2,128)S(1)}, u32[]{:S(2)}, u32[]{:S(2)}) collective-permute-start(f32[256,2,128]{2,1,0:T(2,128)S(1)} %constant_dynamic-slice_fusion.5), channel_id=1, source_target_pairs={{0,1},{1,0},{2,3},{3,2},{4,5},{5,4},{6,7},{7,6},{8,9},{9,8},{10,11... | collective-permute-start | bytes 786440 | tf_op jit(solution)/shard_map/ppermute | solution.py:438
  48.1 6.8 %collective-permute-start.7 = (f32[64,2048]{1,0:T(8,128)S(1)}, f32[64,2048]{1,0:T(8,128)S(1)}, u32[]{:S(2)}, u32[]{:S(2)}) collective-permute-start(f32[64,2048]{1,0:T(8,128)S(1)} %constant_dynamic-slice_fusion.2), channel_id=1, source_target_pairs={{0,4},{4,0},{8,12},{12,8},{16,20},{20,16},{24,28},{28,24},{1,5},{5... | collective-permute-start | bytes 1572872 | tf_op jit(solution)/shard_map/ppermute | solution.py:438
  51.5 19.5 %collective-permute-start.2 = (f32[128,2,128]{2,1,0:T(2,128)S(1)}, f32[128,2,128]{2,1,0:T(2,128)S(1)}, u32[]{:S(2)}, u32[]{:S(2)}) collective-permute-start(f32[128,2,128]{2,1,0:T(2,128)S(1)} %constant_dynamic-slice_fusion.4), channel_id=1, source_target_pairs={{0,2},{1,3},{2,0},{3,1},{4,6},{5,7},{6,4},{7,5},{8,10},{9,11},{10,... | collective-permute-start | bytes 393224 | tf_op jit(solution)/shard_map/ppermute | solution.py:438
  55.0 18.1 %collective-permute-start.8 = (f32[16,2048]{1,0:T(8,128)S(1)}, f32[16,2048]{1,0:T(8,128)S(1)}, u32[]{:S(2)}, u32[]{:S(2)}) collective-permute-start(f32[16,2048]{1,0:T(8,128)S(1)} %get-tuple-element.52), channel_id=1, source_target_pairs={{0,8},{4,12},{8,0},{12,4},{16,24},{20,28},{24,16},{28,20},{1,9},{5... | collective-permute-start | bytes 393224 | tf_op jit(solution)/shard_map/ppermute | solution.py:438
  55.5 19.6 %collective-permute-start.10 = (f32[16,2048]{1,0:T(8,128)S(1)}, f32[16,2048]{1,0:T(8,128)S(1)}, u32[]{:S(2)}, u32[]{:S(2)}) collective-permute-start(f32[16,2048]{1,0:T(8,128)S(1)} %get-tuple-element.53), channel_id=1, source_target_pairs={{0,24},{4,28},{8,16},{12,20},{16,8},{20,12},{24,0},{28,4},{1,25},{... | collective-permute-start | bytes 393224 | tf_op jit(solution)/shard_map/ppermute | solution.py:438
  70.4 6.0 %collective-permute-start.9 = (f32[16,2048]{1,0:T(8,128)S(1)}, f32[16,2048]{1,0:T(8,128)S(1)}, u32[]{:S(2)}, u32[]{:S(2)}) collective-permute-start(f32[16,2048]{1,0:T(8,128)S(1)} %get-tuple-element.54), channel_id=1, source_target_pairs={{0,16},{4,20},{8,24},{12,28},{16,0},{20,4},{24,8},{28,12},{1,17},{... | collective-permute-start | bytes 393224 | tf_op jit(solution)/shard_map/ppermute | solution.py:438
  72.1 7.9 %collective-permute-start.3 = (f32[128,2,128]{2,1,0:T(2,128)S(1)}, f32[128,2,128]{2,1,0:T(2,128)S(1)}, u32[]{:S(2)}, u32[]{:S(2)}) collective-permute-start(f32[128,2,128]{2,1,0:T(2,128)S(1)} %multiply_multiply_fusion.1), channel_id=1, source_target_pairs={{0,2},{1,3},{2,0},{3,1},{4,6},{5,7},{6,4},{7,5},{8,10},{9,11},{10,... | collective-permute-start | bytes 393224 | tf_op jit(solution)/shard_map/ppermute | solution.py:438
  76.4 6.3 %collective-permute-start.13 = (f32[16,2048]{1,0:T(8,128)S(1)}, f32[16,2048]{1,0:T(8,128)S(1)}, u32[]{:S(2)}, u32[]{:S(2)}) collective-permute-start(f32[16,2048]{1,0:T(8,128)S(1)} %fusion.6), channel_id=1, source_target_pairs={{0,8},{4,12},{8,0},{12,4},{16,24},{20,28},{24,16},{28,20},{1,9},{5... | collective-permute-start | bytes 393224 | tf_op jit(solution)/shard_map/ppermute | solution.py:438
  78.3 7.6 %collective-permute-start.12 = (f32[16,2048]{1,0:T(8,128)S(1)}, f32[16,2048]{1,0:T(8,128)S(1)}, u32[]{:S(2)}, u32[]{:S(2)}) collective-permute-start(f32[16,2048]{1,0:T(8,128)S(1)} %fusion.6), channel_id=1, source_target_pairs={{0,16},{4,20},{8,24},{12,28},{16,0},{20,4},{24,8},{28,12},{1,17},{... | collective-permute-start | bytes 393224 | tf_op jit(solution)/shard_map/ppermute | solution.py:438
  78.5 7.4 %collective-permute-start.11 = (f32[16,2048]{1,0:T(8,128)S(1)}, f32[16,2048]{1,0:T(8,128)S(1)}, u32[]{:S(2)}, u32[]{:S(2)}) collective-permute-start(f32[16,2048]{1,0:T(8,128)S(1)} %fusion.6), channel_id=1, source_target_pairs={{0,24},{4,28},{8,16},{12,20},{16,8},{20,12},{24,0},{28,4},{1,25},{... | collective-permute-start | bytes 393224 | tf_op jit(solution)/shard_map/ppermute | solution.py:438
  80.2 7.7 %collective-permute-start.4 = (f32[256,2,128]{2,1,0:T(2,128)S(1)}, f32[256,2,128]{2,1,0:T(2,128)}, u32[]{:S(2)}, u32[]{:S(2)}) collective-permute-start(f32[256,2,128]{2,1,0:T(2,128)S(1)} %pad_maximum_fusion.6), channel_id=1, source_target_pairs={{0,1},{1,0},{2,3},{3,2},{4,5},{5,4},{6,7},{7,6},{8,9},{9,8},{10,11... | collective-permute-start | bytes 786440 | tf_op jit(solution)/shard_map/ppermute | solution.py:438
  86.0 3.1 %collective-permute-start.14 = (f32[64,2048]{1,0:T(8,128)S(1)}, f32[64,2048]{1,0:T(8,128)S(1)}, u32[]{:S(2)}, u32[]{:S(2)}) collective-permute-start(f32[64,2048]{1,0:T(8,128)S(1)} %pad_maximum_fusion.3), channel_id=1, source_target_pairs={{0,4},{4,0},{8,12},{12,8},{16,20},{20,16},{24,28},{28,24},{1,5},{5... | collective-permute-start | bytes 1572872 | tf_op jit(solution)/shard_map/ppermute | solution.py:438
  86.2 9.8 %collective-permute-start.5 = (f32[16,2048]{1,0:T(8,128)S(1)}, f32[16,2048]{1,0:T(8,128)S(1)}, u32[]{:S(2)}, u32[]{:S(2)}) collective-permute-start(f32[16,2048]{1,0:T(8,128)S(1)} %get-tuple-element.20), channel_id=1, source_target_pairs={{0,1},{1,2},{2,3},{4,5},{5,6},{6,7},{8,9},{9,10},{10,11},{12,13},{... | collective-permute-start | bytes 393224 | tf_op jit(solution)/shard_map/ppermute | solution.py:31
  89.3 6.7 %collective-permute-start.15 = (f32[1,2048]{1,0:T(1,128)S(1)}, f32[1,2048]{1,0:T(1,128)S(1)}, u32[]{:S(2)}, u32[]{:S(2)}) collective-permute-start(f32[1,2048]{1,0:T(1,128)S(1)} %slice_bitcast_fusion), channel_id=1, source_target_pairs={{0,1},{1,2},{2,3},{4,5},{5,6},{6,7},{8,9},{9,10},{10,11},{12,13},{... | collective-permute-start | bytes 24584 | tf_op jit(solution)/shard_map/ppermute | solution.py:31
  127.2 8.3 %collective-permute-start.16 = (f32[16,2048]{1,0:T(8,128)S(1)}, f32[16,2048]{1,0:T(8,128)S(1)}, u32[]{:S(2)}, u32[]{:S(2)}) collective-permute-start(f32[16,2048]{1,0:T(8,128)S(1)} %get-tuple-element.26), channel_id=1, source_target_pairs={{1,0},{2,1},{3,2},{5,4},{6,5},{7,6},{9,8},{10,9},{11,10},{13,12},{... | collective-permute-start | bytes 393224 | tf_op jit(solution)/shard_map/ppermute | solution.py:31
  128.5 10.7 %collective-permute-start.25 = (f32[256,2,128]{2,1,0:T(2,128)S(1)}, f32[256,2,128]{2,1,0:T(2,128)S(1)}, u32[]{:S(2)}, u32[]{:S(2)}) collective-permute-start(f32[256,2,128]{2,1,0:T(2,128)S(1)} %constant_dynamic-slice_fusion.6), channel_id=1, source_target_pairs={{0,1},{1,0},{2,3},{3,2},{4,5},{5,4},{6,7},{7,6},{8,9},{9,8},{10,11... | collective-permute-start | bytes 786440 | tf_op jit(solution)/shard_map/ppermute | solution.py:438
  135.8 38.4 %slice-start = ((s8[8388608]{0:T(1024)(128)(4,1)}), s8[4194304]{0:T(1024)(128)(4,1)S(1)}, s32[]{:S(2)}) async-start(s8[8388608]{0:T(1024)(128)(4,1)} %bitcast.61), calls=%async_computation | async-start | bytes 8388608
  135.8 5.4 %collective-permute-start.17 = (f32[64,2048]{1,0:T(8,128)S(1)}, f32[64,2048]{1,0:T(8,128)S(1)}, u32[]{:S(2)}, u32[]{:S(2)}) collective-permute-start(f32[64,2048]{1,0:T(8,128)S(1)} %constant_dynamic-slice_fusion.1), channel_id=1, source_target_pairs={{0,4},{4,0},{8,12},{12,8},{16,20},{20,16},{24,28},{28,24},{1,5},{5... | collective-permute-start | bytes 1572872 | tf_op jit(solution)/shard_map/ppermute | solution.py:438
  139.4 17.9 %collective-permute-start.26 = (f32[128,2,128]{2,1,0:T(2,128)S(1)}, f32[128,2,128]{2,1,0:T(2,128)S(1)}, u32[]{:S(2)}, u32[]{:S(2)}) collective-permute-start(f32[128,2,128]{2,1,0:T(2,128)S(1)} %constant_dynamic-slice_fusion), channel_id=1, source_target_pairs={{0,2},{1,3},{2,0},{3,1},{4,6},{5,7},{6,4},{7,5},{8,10},{9,11},{10,... | collective-permute-start | bytes 393224 | tf_op jit(solution)/shard_map/ppermute | solution.py:438
  141.3 18.7 %collective-permute-start.18 = (f32[16,2048]{1,0:T(8,128)S(1)}, f32[16,2048]{1,0:T(8,128)S(1)}, u32[]{:S(2)}, u32[]{:S(2)}) collective-permute-start(f32[16,2048]{1,0:T(8,128)S(1)} %get-tuple-element.45), channel_id=1, source_target_pairs={{0,8},{4,12},{8,0},{12,4},{16,24},{20,28},{24,16},{28,20},{1,9},{5... | collective-permute-start | bytes 393224 | tf_op jit(solution)/shard_map/ppermute | solution.py:438
  141.4 19.8 %collective-permute-start.20 = (f32[16,2048]{1,0:T(8,128)S(1)}, f32[16,2048]{1,0:T(8,128)S(1)}, u32[]{:S(2)}, u32[]{:S(2)}) collective-permute-start(f32[16,2048]{1,0:T(8,128)S(1)} %get-tuple-element.46), channel_id=1, source_target_pairs={{0,24},{4,28},{8,16},{12,20},{16,8},{20,12},{24,0},{28,4},{1,25},{... | collective-permute-start | bytes 393224 | tf_op jit(solution)/shard_map/ppermute | solution.py:438
  156.8 5.7 %collective-permute-start.19 = (f32[16,2048]{1,0:T(8,128)S(1)}, f32[16,2048]{1,0:T(8,128)S(1)}, u32[]{:S(2)}, u32[]{:S(2)}) collective-permute-start(f32[16,2048]{1,0:T(8,128)S(1)} %get-tuple-element.47), channel_id=1, source_target_pairs={{0,16},{4,20},{8,24},{12,28},{16,0},{20,4},{24,8},{28,12},{1,17},{... | collective-permute-start | bytes 393224 | tf_op jit(solution)/shard_map/ppermute | solution.py:438
  158.6 7.5 %collective-permute-start.27 = (f32[128,2,128]{2,1,0:T(2,128)S(1)}, f32[128,2,128]{2,1,0:T(2,128)S(1)}, u32[]{:S(2)}, u32[]{:S(2)}) collective-permute-start(f32[128,2,128]{2,1,0:T(2,128)S(1)} %multiply_multiply_fusion), channel_id=1, source_target_pairs={{0,2},{1,3},{2,0},{3,1},{4,6},{5,7},{6,4},{7,5},{8,10},{9,11},{10,... | collective-permute-start | bytes 393224 | tf_op jit(solution)/shard_map/ppermute | solution.py:438
  162.6 5.6 %collective-permute-start.23 = (f32[16,2048]{1,0:T(8,128)S(1)}, f32[16,2048]{1,0:T(8,128)S(1)}, u32[]{:S(2)}, u32[]{:S(2)}) collective-permute-start(f32[16,2048]{1,0:T(8,128)S(1)} %fusion.4), channel_id=1, source_target_pairs={{0,8},{4,12},{8,0},{12,4},{16,24},{20,28},{24,16},{28,20},{1,9},{5... | collective-permute-start | bytes 393224 | tf_op jit(solution)/shard_map/ppermute | solution.py:438
  164.6 6.8 %collective-permute-start.22 = (f32[16,2048]{1,0:T(8,128)S(1)}, f32[16,2048]{1,0:T(8,128)S(1)}, u32[]{:S(2)}, u32[]{:S(2)}) collective-permute-start(f32[16,2048]{1,0:T(8,128)S(1)} %fusion.4), channel_id=1, source_target_pairs={{0,16},{4,20},{8,24},{12,28},{16,0},{20,4},{24,8},{28,12},{1,17},{... | collective-permute-start | bytes 393224 | tf_op jit(solution)/shard_map/ppermute | solution.py:438
  164.8 6.7 %collective-permute-start.21 = (f32[16,2048]{1,0:T(8,128)S(1)}, f32[16,2048]{1,0:T(8,128)S(1)}, u32[]{:S(2)}, u32[]{:S(2)}) collective-permute-start(f32[16,2048]{1,0:T(8,128)S(1)} %fusion.4), channel_id=1, source_target_pairs={{0,24},{4,28},{8,16},{12,20},{16,8},{20,12},{24,0},{28,4},{1,25},{... | collective-permute-start | bytes 393224 | tf_op jit(solution)/shard_map/ppermute | solution.py:438
  166.3 7.9 %slice-start.1 = ((s8[8388608]{0:T(1024)(128)(4,1)}), s8[4194304]{0:T(1024)(128)(4,1)S(1)}, s32[]{:S(2)}) async-start(s8[8388608]{0:T(1024)(128)(4,1)} %bitcast.61), calls=%async_computation.1 | async-start | bytes 8388608
  166.3 6.4 %collective-permute-start.28 = (f32[256,2,128]{2,1,0:T(2,128)S(1)}, f32[256,2,128]{2,1,0:T(2,128)S(1)}, u32[]{:S(2)}, u32[]{:S(2)}) collective-permute-start(f32[256,2,128]{2,1,0:T(2,128)S(1)} %pad_maximum_fusion.7), channel_id=1, source_target_pairs={{0,1},{1,0},{2,3},{3,2},{4,5},{5,4},{6,7},{7,6},{8,9},{9,8},{10,11... | collective-permute-start | bytes 786440 | tf_op jit(solution)/shard_map/ppermute | solution.py:438
  171.6 2.4 %collective-permute-start.24 = (f32[64,2048]{1,0:T(8,128)S(1)}, f32[64,2048]{1,0:T(8,128)S(1)}, u32[]{:S(2)}, u32[]{:S(2)}) collective-permute-start(f32[64,2048]{1,0:T(8,128)S(1)} %pad_maximum_fusion.4), channel_id=1, source_target_pairs={{0,4},{4,0},{8,12},{12,8},{16,20},{20,16},{24,28},{28,24},{1,5},{5... | collective-permute-start | bytes 1572872 | tf_op jit(solution)/shard_map/ppermute | solution.py:438

commit v4 on v3

--- a/solution.py
+++ b/solution.py
@@ -18,8 +18,8 @@
 RADIUS = 12.0
 ROOT_HALF = 0.7071067811865476
 
-GROUP = 8
-RING = 36
+GROUP = 16
+RING = 18
 CHUNK = 352
 PIECE = 512
 DEPTH = 3

time: 185 us -> 179 us (0.968)
  starting transfers between devices: 67.4 us -> 63.1 us
  Pallas kernels: 68.5 us -> 64.9 us
    pallas_call x2, Pallas kernels: 59 us -> 55.4 us  [iteration(): pl.pallas_call(functools.partial(iteration_kernel, first, dims), out_shap...]
    ppermute x24, starting transfers between devices: 52.8 us -> 49.8 us  [exchange(): return lax.ppermute(value, axis, [(i, i ^ bit) for i in range(count)])]
where the time goes in v4:
time: 179 us; the launch traced here: 178 us
  Pallas kernels  64.9 us (36%)
  starting transfers between devices  63.1 us (35%)
  waiting for transfers between devices  34.6 us (19%)
  other arithmetic  9.77 us (5%)
  local copies, waits for them, and re-layouts  3.89 us (2%)
    pallas_call x2, Pallas kernels, iteration(): pl.pallas_call(functools.partial(iteration_kernel, first, dims), out_shap...  55.4 us
    ppermute x24, starting transfers between devices, exchange(): return lax.ppermute(value, axis, [(i, i ^ bit) for i in range(count)])  49.8 us
    ppermute x24, waiting for transfers between devices, exchange(): return lax.ppermute(value, axis, [(i, i ^ bit) for i in range(count)])  25.3 us
    ppermute x5, starting transfers between devices, shifted(): return lax.ppermute(shard, axis, pairs)  13.3 us
    pallas_call x1, Pallas kernels, shrink(): pl.pallas_call(shrink_kernel, out_shape=jax.ShapeDtypeStruct(push.shape,...  9.53 us
    ppermute x5, waiting for transfers between devices, shifted(): return lax.ppermute(shard, axis, pairs)  9.3 us
  transfers between devices with their start and end apart: 29, of which 14 were waited for; matrix products, arithmetic and copies ran while one was open for 7% of the time, Pallas kernels for 0%

profile of v4, /device:TPU:0, one launch (start us, length us, event | category | flops | bytes accessed | tf_op | source)
XLA Modules:
  0.0 177.5 jit_solution(8447658200553968302)
XLA Ops:
  0.6 1.3 slice.26
  2.0 4.9 %collective-permute-start = (f32[16,2048]{1,0:T(8,128)S(1)}, f32[16,2048]{1,0:T(8,128)S(1)}, u32[]{:S(2)}, u32[]{:S(2)}) collective-permute-start(f32[16,2048]{1,0:T(8,128)S(1)} %bitcast.93), channel_id=1, source_target_pairs={{0,1},{1,2},{2,3},{4,5},{5,6},{6,7},{8,9},{9,10},{10,11},{12,13},{... | collective-permute-start | bytes 393224 | tf_op jit(solution)/shard_map/ppermute | solution.py:31
  11.6 26.4 %primal_dual_first.1 = (f32[16,64,2048]{2,1,0:T(8,128)}, f32[16,2,64,2048]{3,2,1,0:T(8,128)}, f32[2,64,2048]{2,1,0:T(8,128)S(1)}, f32[512,2,128]{2,1,0:T(2,128)S...) custom-call(s32[1024]{0:T(1024)S(1)} %select_reduce_fusion.refs_0_, ...), custom_call_target="tpu_custom_call" | custom-call | tf_op jit(solution)/shard_map/primal_dual_first/pallas_call | solution.py:375
  38.0 1.3 collective-permute-start.6
  39.5 2.7 %collective-permute-start.1 = (f32[256,2,128]{2,1,0:T(2,128)S(1)}, f32[256,2,128]{2,1,0:T(2,128)S(1)}, u32[]{:S(2)}, u32[]{:S(2)}) collective-permute-start(f32[256,2,128]{2,1,0:T(2,128)S(1)} %constant_dynamic-slice_fusion.5), channel_id=1, source_target_pairs={{0,1},{1,0},{2,3},{3,2},{4,5},{5,4},{6,7},{7,6},{8,9},{9,8},{10,11... | collective-permute-start | bytes 786440 | tf_op jit(solution)/shard_map/ppermute | solution.py:438
  42.2 4.1 %collective-permute-done.6 = f32[16,2048]{1,0:T(8,128)S(1)} collective-permute-done((f32[16,2048]{1,0:T(8,128)S(1)}, f32[16,2048]{1,0:T(8,128)S(1)}, u32[]{:S(2)}, u32[]{:S(2)}) %collective-permute-start.6) | collective-permute-done | bytes 131104 | tf_op jit(solution)/shard_map/ppermute | solution.py:31
  46.9 3.3 %collective-permute-done.1 = f32[256,2,128]{2,1,0:T(2,128)S(1)} collective-permute-done((f32[256,2,128]{2,1,0:T(2,128)S(1)}, f32[256,2,128]{2,1,0:T(2,128)S(1)}, u32[]{:S(2)}, u32[]{:S(2)}) %collective-permute-start.1) | collective-permute-done | bytes 262176 | tf_op jit(solution)/shard_map/ppermute | solution.py:438
  50.3 3.7 %collective-permute-start.2 = (f32[128,2,128]{2,1,0:T(2,128)S(1)}, f32[128,2,128]{2,1,0:T(2,128)S(1)}, u32[]{:S(2)}, u32[]{:S(2)}) collective-permute-start(f32[128,2,128]{2,1,0:T(2,128)S(1)} %constant_dynamic-slice_fusion.4), channel_id=1, source_target_pairs={{0,2},{1,3},{2,0},{3,1},{4,6},{5,7},{6,4},{7,5},{8,10},{9,11},{10,... | collective-permute-start | bytes 393224 | tf_op jit(solution)/shard_map/ppermute | solution.py:438
  54.2 14.9 %collective-permute-start.10 = (f32[16,2048]{1,0:T(8,128)S(1)}, f32[16,2048]{1,0:T(8,128)S(1)}, u32[]{:S(2)}, u32[]{:S(2)}) collective-permute-start(f32[16,2048]{1,0:T(8,128)S(1)} %get-tuple-element.53), channel_id=1, source_target_pairs={{0,24},{4,28},{8,16},{12,20},{16,8},{20,12},{24,0},{28,4},{1,25},{... | collective-permute-start | bytes 393224 | tf_op jit(solution)/shard_map/ppermute | solution.py:438
  70.8 3.0 %collective-permute-done.10 = f32[16,2048]{1,0:T(8,128)S(1)} collective-permute-done((f32[16,2048]{1,0:T(8,128)S(1)}, f32[16,2048]{1,0:T(8,128)S(1)}, u32[]{:S(2)}, u32[]{:S(2)}) %collective-permute-start.10) | collective-permute-done | bytes 131104 | tf_op jit(solution)/shard_map/ppermute | solution.py:438
  73.8 1.3 collective-permute-done.9
  75.2 1.9 %collective-permute-start.13 = (f32[16,2048]{1,0:T(8,128)S(1)}, f32[16,2048]{1,0:T(8,128)S(1)}, u32[]{:S(2)}, u32[]{:S(2)}) collective-permute-start(f32[16,2048]{1,0:T(8,128)S(1)} %fusion.6), channel_id=1, source_target_pairs={{0,8},{4,12},{8,0},{12,4},{16,24},{20,28},{24,16},{28,20},{1,9},{5... | collective-permute-start | bytes 393224 | tf_op jit(solution)/shard_map/ppermute | solution.py:438
  77.1 1.6 collective-permute-start.11
  79.0 1.4 collective-permute-done.13
  80.4 3.4 %collective-permute-done.12 = f32[16,2048]{1,0:T(8,128)S(1)} collective-permute-done((f32[16,2048]{1,0:T(8,128)S(1)}, f32[16,2048]{1,0:T(8,128)S(1)}, u32[]{:S(2)}, u32[]{:S(2)}) %collective-permute-start.12) | collective-permute-done | bytes 131104 | tf_op jit(solution)/shard_map/ppermute | solution.py:438
  84.1 2.6 %collective-permute-start.5 = (f32[16,2048]{1,0:T(8,128)S(1)}, f32[16,2048]{1,0:T(8,128)S(1)}, u32[]{:S(2)}, u32[]{:S(2)}) collective-permute-start(f32[16,2048]{1,0:T(8,128)S(1)} %get-tuple-element.20), channel_id=1, source_target_pairs={{0,1},{1,2},{2,3},{4,5},{5,6},{6,7},{8,9},{9,10},{10,11},{12,13},{... | collective-permute-start | bytes 393224 | tf_op jit(solution)/shard_map/ppermute | solution.py:31
  88.2 3.2 %collective-permute-start.15 = (f32[1,2048]{1,0:T(1,128)S(1)}, f32[1,2048]{1,0:T(1,128)S(1)}, u32[]{:S(2)}, u32[]{:S(2)}) collective-permute-start(f32[1,2048]{1,0:T(1,128)S(1)} %slice_bitcast_fusion), channel_id=1, source_target_pairs={{0,1},{1,2},{2,3},{4,5},{5,6},{6,7},{8,9},{9,10},{10,11},{12,13},{... | collective-permute-start | bytes 24584 | tf_op jit(solution)/shard_map/ppermute | solution.py:31
  92.6 29.0 %primal_dual_next.1 = (f32[16,64,2048]{2,1,0:T(8,128)}, bf16[16,2,64,2048]{3,2,1,0:T(8,128)(2,1)}, f32[2,64,2048]{2,1,0:T(8,128)S(1)}, f32[512,2,128]{2,1,0:T(2,...) custom-call(s32[1024]{0:T(1024)S(1)} %select_reduce_fusion.refs_0_, ...), custom_call_target="tpu_custom_call" | custom-call | tf_op jit(solution)/shard_map/primal_dual_next/pallas_call | solution.py:375
  121.6 1.3 collective-permute-start.16
  123.0 2.9 %collective-permute-start.25 = (f32[256,2,128]{2,1,0:T(2,128)S(1)}, f32[256,2,128]{2,1,0:T(2,128)S(1)}, u32[]{:S(2)}, u32[]{:S(2)}) collective-permute-start(f32[256,2,128]{2,1,0:T(2,128)S(1)} %constant_dynamic-slice_fusion.6), channel_id=1, source_target_pairs={{0,1},{1,0},{2,3},{3,2},{4,5},{5,4},{6,7},{7,6},{8,9},{9,8},{10,11... | collective-permute-start | bytes 786440 | tf_op jit(solution)/shard_map/ppermute | solution.py:438
  125.9 4.3 %collective-permute-done.16 = f32[16,2048]{1,0:T(8,128)S(1)} collective-permute-done((f32[16,2048]{1,0:T(8,128)S(1)}, f32[16,2048]{1,0:T(8,128)S(1)}, u32[]{:S(2)}, u32[]{:S(2)}) %collective-permute-start.16) | collective-permute-done | bytes 131104 | tf_op jit(solution)/shard_map/ppermute | solution.py:31
  130.6 3.6 %collective-permute-done.25 = f32[256,2,128]{2,1,0:T(2,128)S(1)} collective-permute-done((f32[256,2,128]{2,1,0:T(2,128)S(1)}, f32[256,2,128]{2,1,0:T(2,128)S(1)}, u32[]{:S(2)}, u32[]{:S(2)}) %collective-permute-start.25) | collective-permute-done | bytes 262176 | tf_op jit(solution)/shard_map/ppermute | solution.py:438
  134.3 1.7 collective-permute-start.26
  136.4 13.7 %collective-permute-start.20 = (f32[16,2048]{1,0:T(8,128)S(1)}, f32[16,2048]{1,0:T(8,128)S(1)}, u32[]{:S(2)}, u32[]{:S(2)}) collective-permute-start(f32[16,2048]{1,0:T(8,128)S(1)} %get-tuple-element.46), channel_id=1, source_target_pairs={{0,24},{4,28},{8,16},{12,20},{16,8},{20,12},{24,0},{28,4},{1,25},{... | collective-permute-start | bytes 393224 | tf_op jit(solution)/shard_map/ppermute | solution.py:438
  150.6 1.3 multiply_multiply_fusion
  152.6 1.8 %collective-permute-done.20 = f32[16,2048]{1,0:T(8,128)S(1)} collective-permute-done((f32[16,2048]{1,0:T(8,128)S(1)}, f32[16,2048]{1,0:T(8,128)S(1)}, u32[]{:S(2)}, u32[]{:S(2)}) %collective-permute-start.20) | collective-permute-done | bytes 131104 | tf_op jit(solution)/shard_map/ppermute | solution.py:438
  154.4 1.3 collective-permute-done.19
  155.8 2.6 %collective-permute-start.23 = (f32[16,2048]{1,0:T(8,128)S(1)}, f32[16,2048]{1,0:T(8,128)S(1)}, u32[]{:S(2)}, u32[]{:S(2)}) collective-permute-start(f32[16,2048]{1,0:T(8,128)S(1)} %fusion.4), channel_id=1, source_target_pairs={{0,8},{4,12},{8,0},{12,4},{16,24},{20,28},{24,16},{28,20},{1,9},{5... | collective-permute-start | bytes 393224 | tf_op jit(solution)/shard_map/ppermute | solution.py:438
  158.4 1.5 collective-permute-start.21
  161.3 3.4 %collective-permute-done.22 = f32[16,2048]{1,0:T(8,128)S(1)} collective-permute-done((f32[16,2048]{1,0:T(8,128)S(1)}, f32[16,2048]{1,0:T(8,128)S(1)}, u32[]{:S(2)}, u32[]{:S(2)}) %collective-permute-start.22) | collective-permute-done | bytes 131104 | tf_op jit(solution)/shard_map/ppermute | solution.py:438
  164.9 1.6 collective-permute-done.28
  168.0 9.5 %shrink.1 = f32[16,2,64,2048]{3,2,1,0:T(8,128)} custom-call(bf16[16,2,64,2048]{3,2,1,0:T(8,128)(2,1)S(1)} %bitcast.62, f32[16,2048]{1,0:T(8,128)S(1)} %get-tuple-element.30.last_ref, f32[2,64,2048]{2,1,0:T(8,128)S(1)} %bitcast.65, f32[64,1]{1,0:T(8,128)S(1)} %copy.27.refs_9_.rad_ref), custom_call_target="tpu_custom_call" | custom-call | tf_op jit(solution)/shard_map/shrink/pallas_call | solution.py:422
  (94 shorter events, 15.7 us)
Async XLA Ops:
  2.0 9.5 %collective-permute-start = (f32[16,2048]{1,0:T(8,128)S(1)}, f32[16,2048]{1,0:T(8,128)S(1)}, u32[]{:S(2)}, u32[]{:S(2)}) collective-permute-start(f32[16,2048]{1,0:T(8,128)S(1)} %bitcast.93), channel_id=1, source_target_pairs={{0,1},{1,2},{2,3},{4,5},{5,6},{6,7},{8,9},{9,10},{10,11},{12,13},{... | collective-permute-start | bytes 393224 | tf_op jit(solution)/shard_map/ppermute | solution.py:31
  38.0 8.3 %collective-permute-start.6 = (f32[16,2048]{1,0:T(8,128)S(1)}, f32[16,2048]{1,0:T(8,128)S(1)}, u32[]{:S(2)}, u32[]{:S(2)}) collective-permute-start(f32[16,2048]{1,0:T(8,128)S(1)} %get-tuple-element.19), channel_id=1, source_target_pairs={{1,0},{2,1},{3,2},{5,4},{6,5},{7,6},{9,8},{10,9},{11,10},{13,12},{... | collective-permute-start | bytes 393224 | tf_op jit(solution)/shard_map/ppermute | solution.py:31
  39.5 10.6 %collective-permute-start.1 = (f32[256,2,128]{2,1,0:T(2,128)S(1)}, f32[256,2,128]{2,1,0:T(2,128)S(1)}, u32[]{:S(2)}, u32[]{:S(2)}) collective-permute-start(f32[256,2,128]{2,1,0:T(2,128)S(1)} %constant_dynamic-slice_fusion.5), channel_id=1, source_target_pairs={{0,1},{1,0},{2,3},{3,2},{4,5},{5,4},{6,7},{7,6},{8,9},{9,8},{10,11... | collective-permute-start | bytes 786440 | tf_op jit(solution)/shard_map/ppermute | solution.py:438
  46.6 7.4 %collective-permute-start.7 = (f32[64,2048]{1,0:T(8,128)S(1)}, f32[64,2048]{1,0:T(8,128)S(1)}, u32[]{:S(2)}, u32[]{:S(2)}) collective-permute-start(f32[64,2048]{1,0:T(8,128)S(1)} %constant_dynamic-slice_fusion.2), channel_id=1, source_target_pairs={{0,4},{4,0},{8,12},{12,8},{16,20},{20,16},{24,28},{28,24},{1,5},{5... | collective-permute-start | bytes 1572872 | tf_op jit(solution)/shard_map/ppermute | solution.py:438
  50.3 19.2 %collective-permute-start.2 = (f32[128,2,128]{2,1,0:T(2,128)S(1)}, f32[128,2,128]{2,1,0:T(2,128)S(1)}, u32[]{:S(2)}, u32[]{:S(2)}) collective-permute-start(f32[128,2,128]{2,1,0:T(2,128)S(1)} %constant_dynamic-slice_fusion.4), channel_id=1, source_target_pairs={{0,2},{1,3},{2,0},{3,1},{4,6},{5,7},{6,4},{7,5},{8,10},{9,11},{10,... | collective-permute-start | bytes 393224 | tf_op jit(solution)/shard_map/ppermute | solution.py:438
  54.1 16.7 %collective-permute-start.8 = (f32[16,2048]{1,0:T(8,128)S(1)}, f32[16,2048]{1,0:T(8,128)S(1)}, u32[]{:S(2)}, u32[]{:S(2)}) collective-permute-start(f32[16,2048]{1,0:T(8,128)S(1)} %get-tuple-element.52), channel_id=1, source_target_pairs={{0,8},{4,12},{8,0},{12,4},{16,24},{20,28},{24,16},{28,20},{1,9},{5... | collective-permute-start | bytes 393224 | tf_op jit(solution)/shard_map/ppermute | solution.py:438
  54.2 19.6 %collective-permute-start.10 = (f32[16,2048]{1,0:T(8,128)S(1)}, f32[16,2048]{1,0:T(8,128)S(1)}, u32[]{:S(2)}, u32[]{:S(2)}) collective-permute-start(f32[16,2048]{1,0:T(8,128)S(1)} %get-tuple-element.53), channel_id=1, source_target_pairs={{0,24},{4,28},{8,16},{12,20},{16,8},{20,12},{24,0},{28,4},{1,25},{... | collective-permute-start | bytes 393224 | tf_op jit(solution)/shard_map/ppermute | solution.py:438
  69.1 6.1 %collective-permute-start.9 = (f32[16,2048]{1,0:T(8,128)S(1)}, f32[16,2048]{1,0:T(8,128)S(1)}, u32[]{:S(2)}, u32[]{:S(2)}) collective-permute-start(f32[16,2048]{1,0:T(8,128)S(1)} %get-tuple-element.54), channel_id=1, source_target_pairs={{0,16},{4,20},{8,24},{12,28},{16,0},{20,4},{24,8},{28,12},{1,17},{... | collective-permute-start | bytes 393224 | tf_op jit(solution)/shard_map/ppermute | solution.py:438
  70.7 8.0 %collective-permute-start.3 = (f32[128,2,128]{2,1,0:T(2,128)S(1)}, f32[128,2,128]{2,1,0:T(2,128)S(1)}, u32[]{:S(2)}, u32[]{:S(2)}) collective-permute-start(f32[128,2,128]{2,1,0:T(2,128)S(1)} %multiply_multiply_fusion.1), channel_id=1, source_target_pairs={{0,2},{1,3},{2,0},{3,1},{4,6},{5,7},{6,4},{7,5},{8,10},{9,11},{10,... | collective-permute-start | bytes 393224 | tf_op jit(solution)/shard_map/ppermute | solution.py:438
  75.2 5.2 %collective-permute-start.13 = (f32[16,2048]{1,0:T(8,128)S(1)}, f32[16,2048]{1,0:T(8,128)S(1)}, u32[]{:S(2)}, u32[]{:S(2)}) collective-permute-start(f32[16,2048]{1,0:T(8,128)S(1)} %fusion.6), channel_id=1, source_target_pairs={{0,8},{4,12},{8,0},{12,4},{16,24},{20,28},{24,16},{28,20},{1,9},{5... | collective-permute-start | bytes 393224 | tf_op jit(solution)/shard_map/ppermute | solution.py:438
  77.1 6.6 %collective-permute-start.12 = (f32[16,2048]{1,0:T(8,128)S(1)}, f32[16,2048]{1,0:T(8,128)S(1)}, u32[]{:S(2)}, u32[]{:S(2)}) collective-permute-start(f32[16,2048]{1,0:T(8,128)S(1)} %fusion.6), channel_id=1, source_target_pairs={{0,16},{4,20},{8,24},{12,28},{16,0},{20,4},{24,8},{28,12},{1,17},{... | collective-permute-start | bytes 393224 | tf_op jit(solution)/shard_map/ppermute | solution.py:438
  77.1 6.6 %collective-permute-start.11 = (f32[16,2048]{1,0:T(8,128)S(1)}, f32[16,2048]{1,0:T(8,128)S(1)}, u32[]{:S(2)}, u32[]{:S(2)}) collective-permute-start(f32[16,2048]{1,0:T(8,128)S(1)} %fusion.6), channel_id=1, source_target_pairs={{0,24},{4,28},{8,16},{12,20},{16,8},{20,12},{24,0},{28,4},{1,25},{... | collective-permute-start | bytes 393224 | tf_op jit(solution)/shard_map/ppermute | solution.py:438
  78.9 7.8 %collective-permute-start.4 = (f32[256,2,128]{2,1,0:T(2,128)S(1)}, f32[256,2,128]{2,1,0:T(2,128)}, u32[]{:S(2)}, u32[]{:S(2)}) collective-permute-start(f32[256,2,128]{2,1,0:T(2,128)S(1)} %pad_maximum_fusion.6), channel_id=1, source_target_pairs={{0,1},{1,0},{2,3},{3,2},{4,5},{5,4},{6,7},{7,6},{8,9},{9,8},{10,11... | collective-permute-start | bytes 786440 | tf_op jit(solution)/shard_map/ppermute | solution.py:438
  83.8 4.1 %collective-permute-start.14 = (f32[64,2048]{1,0:T(8,128)S(1)}, f32[64,2048]{1,0:T(8,128)S(1)}, u32[]{:S(2)}, u32[]{:S(2)}) collective-permute-start(f32[64,2048]{1,0:T(8,128)S(1)} %pad_maximum_fusion.3), channel_id=1, source_target_pairs={{0,4},{4,0},{8,12},{12,8},{16,20},{20,16},{24,28},{28,24},{1,5},{5... | collective-permute-start | bytes 1572872 | tf_op jit(solution)/shard_map/ppermute | solution.py:438
  84.1 8.5 %collective-permute-start.5 = (f32[16,2048]{1,0:T(8,128)S(1)}, f32[16,2048]{1,0:T(8,128)S(1)}, u32[]{:S(2)}, u32[]{:S(2)}) collective-permute-start(f32[16,2048]{1,0:T(8,128)S(1)} %get-tuple-element.20), channel_id=1, source_target_pairs={{0,1},{1,2},{2,3},{4,5},{5,6},{6,7},{8,9},{9,10},{10,11},{12,13},{... | collective-permute-start | bytes 393224 | tf_op jit(solution)/shard_map/ppermute | solution.py:31
  88.2 4.4 %collective-permute-start.15 = (f32[1,2048]{1,0:T(1,128)S(1)}, f32[1,2048]{1,0:T(1,128)S(1)}, u32[]{:S(2)}, u32[]{:S(2)}) collective-permute-start(f32[1,2048]{1,0:T(1,128)S(1)} %slice_bitcast_fusion), channel_id=1, source_target_pairs={{0,1},{1,2},{2,3},{4,5},{5,6},{6,7},{8,9},{9,10},{10,11},{12,13},{... | collective-permute-start | bytes 24584 | tf_op jit(solution)/shard_map/ppermute | solution.py:31
  121.6 8.6 %collective-permute-start.16 = (f32[16,2048]{1,0:T(8,128)S(1)}, f32[16,2048]{1,0:T(8,128)S(1)}, u32[]{:S(2)}, u32[]{:S(2)}) collective-permute-start(f32[16,2048]{1,0:T(8,128)S(1)} %get-tuple-element.26), channel_id=1, source_target_pairs={{1,0},{2,1},{3,2},{5,4},{6,5},{7,6},{9,8},{10,9},{11,10},{13,12},{... | collective-permute-start | bytes 393224 | tf_op jit(solution)/shard_map/ppermute | solution.py:31
  123.0 11.2 %collective-permute-start.25 = (f32[256,2,128]{2,1,0:T(2,128)S(1)}, f32[256,2,128]{2,1,0:T(2,128)S(1)}, u32[]{:S(2)}, u32[]{:S(2)}) collective-permute-start(f32[256,2,128]{2,1,0:T(2,128)S(1)} %constant_dynamic-slice_fusion.6), channel_id=1, source_target_pairs={{0,1},{1,0},{2,3},{3,2},{4,5},{5,4},{6,7},{7,6},{8,9},{9,8},{10,11... | collective-permute-start | bytes 786440 | tf_op jit(solution)/shard_map/ppermute | solution.py:438
  130.5 37.5 %slice-start = ((s8[8388608]{0:T(1024)(128)(4,1)}), s8[4194304]{0:T(1024)(128)(4,1)S(1)}, s32[]{:S(2)}) async-start(s8[8388608]{0:T(1024)(128)(4,1)} %bitcast.61), calls=%async_computation | async-start | bytes 8388608
  130.5 5.5 %collective-permute-start.17 = (f32[64,2048]{1,0:T(8,128)S(1)}, f32[64,2048]{1,0:T(8,128)S(1)}, u32[]{:S(2)}, u32[]{:S(2)}) collective-permute-start(f32[64,2048]{1,0:T(8,128)S(1)} %constant_dynamic-slice_fusion.1), channel_id=1, source_target_pairs={{0,4},{4,0},{8,12},{12,8},{16,20},{20,16},{24,28},{28,24},{1,5},{5... | collective-permute-start | bytes 1572872 | tf_op jit(solution)/shard_map/ppermute | solution.py:438
  134.3 16.2 %collective-permute-start.26 = (f32[128,2,128]{2,1,0:T(2,128)S(1)}, f32[128,2,128]{2,1,0:T(2,128)S(1)}, u32[]{:S(2)}, u32[]{:S(2)}) collective-permute-start(f32[128,2,128]{2,1,0:T(2,128)S(1)} %constant_dynamic-slice_fusion), channel_id=1, source_target_pairs={{0,2},{1,3},{2,0},{3,1},{4,6},{5,7},{6,4},{7,5},{8,10},{9,11},{10,... | collective-permute-start | bytes 393224 | tf_op jit(solution)/shard_map/ppermute | solution.py:438
  136.1 16.4 %collective-permute-start.18 = (f32[16,2048]{1,0:T(8,128)S(1)}, f32[16,2048]{1,0:T(8,128)S(1)}, u32[]{:S(2)}, u32[]{:S(2)}) collective-permute-start(f32[16,2048]{1,0:T(8,128)S(1)} %get-tuple-element.45), channel_id=1, source_target_pairs={{0,8},{4,12},{8,0},{12,4},{16,24},{20,28},{24,16},{28,20},{1,9},{5... | collective-permute-start | bytes 393224 | tf_op jit(solution)/shard_map/ppermute | solution.py:438
  136.4 18.1 %collective-permute-start.20 = (f32[16,2048]{1,0:T(8,128)S(1)}, f32[16,2048]{1,0:T(8,128)S(1)}, u32[]{:S(2)}, u32[]{:S(2)}) collective-permute-start(f32[16,2048]{1,0:T(8,128)S(1)} %get-tuple-element.46), channel_id=1, source_target_pairs={{0,24},{4,28},{8,16},{12,20},{16,8},{20,12},{24,0},{28,4},{1,25},{... | collective-permute-start | bytes 393224 | tf_op jit(solution)/shard_map/ppermute | solution.py:438
  150.1 5.7 %collective-permute-start.19 = (f32[16,2048]{1,0:T(8,128)S(1)}, f32[16,2048]{1,0:T(8,128)S(1)}, u32[]{:S(2)}, u32[]{:S(2)}) collective-permute-start(f32[16,2048]{1,0:T(8,128)S(1)} %get-tuple-element.47), channel_id=1, source_target_pairs={{0,16},{4,20},{8,24},{12,28},{16,0},{20,4},{24,8},{28,12},{1,17},{... | collective-permute-start | bytes 393224 | tf_op jit(solution)/shard_map/ppermute | solution.py:438
  151.9 8.0 %collective-permute-start.27 = (f32[128,2,128]{2,1,0:T(2,128)S(1)}, f32[128,2,128]{2,1,0:T(2,128)S(1)}, u32[]{:S(2)}, u32[]{:S(2)}) collective-permute-start(f32[128,2,128]{2,1,0:T(2,128)S(1)} %multiply_multiply_fusion), channel_id=1, source_target_pairs={{0,2},{1,3},{2,0},{3,1},{4,6},{5,7},{6,4},{7,5},{8,10},{9,11},{10,... | collective-permute-start | bytes 393224 | tf_op jit(solution)/shard_map/ppermute | solution.py:438
  155.8 5.5 %collective-permute-start.23 = (f32[16,2048]{1,0:T(8,128)S(1)}, f32[16,2048]{1,0:T(8,128)S(1)}, u32[]{:S(2)}, u32[]{:S(2)}) collective-permute-start(f32[16,2048]{1,0:T(8,128)S(1)} %fusion.4), channel_id=1, source_target_pairs={{0,8},{4,12},{8,0},{12,4},{16,24},{20,28},{24,16},{28,20},{1,9},{5... | collective-permute-start | bytes 393224 | tf_op jit(solution)/shard_map/ppermute | solution.py:438
  158.4 6.4 %collective-permute-start.22 = (f32[16,2048]{1,0:T(8,128)S(1)}, f32[16,2048]{1,0:T(8,128)S(1)}, u32[]{:S(2)}, u32[]{:S(2)}) collective-permute-start(f32[16,2048]{1,0:T(8,128)S(1)} %fusion.4), channel_id=1, source_target_pairs={{0,16},{4,20},{8,24},{12,28},{16,0},{20,4},{24,8},{28,12},{1,17},{... | collective-permute-start | bytes 393224 | tf_op jit(solution)/shard_map/ppermute | solution.py:438
  158.4 6.4 %collective-permute-start.21 = (f32[16,2048]{1,0:T(8,128)S(1)}, f32[16,2048]{1,0:T(8,128)S(1)}, u32[]{:S(2)}, u32[]{:S(2)}) collective-permute-start(f32[16,2048]{1,0:T(8,128)S(1)} %fusion.4), channel_id=1, source_target_pairs={{0,24},{4,28},{8,16},{12,20},{16,8},{20,12},{24,0},{28,4},{1,25},{... | collective-permute-start | bytes 393224 | tf_op jit(solution)/shard_map/ppermute | solution.py:438
  160.1 7.9 %slice-start.1 = ((s8[8388608]{0:T(1024)(128)(4,1)}), s8[4194304]{0:T(1024)(128)(4,1)S(1)}, s32[]{:S(2)}) async-start(s8[8388608]{0:T(1024)(128)(4,1)} %bitcast.61), calls=%async_computation.1 | async-start | bytes 8388608
  160.1 6.4 %collective-permute-start.28 = (f32[256,2,128]{2,1,0:T(2,128)S(1)}, f32[256,2,128]{2,1,0:T(2,128)S(1)}, u32[]{:S(2)}, u32[]{:S(2)}) collective-permute-start(f32[256,2,128]{2,1,0:T(2,128)S(1)} %pad_maximum_fusion.7), channel_id=1, source_target_pairs={{0,1},{1,0},{2,3},{3,2},{4,5},{5,4},{6,7},{7,6},{8,9},{9,8},{10,11... | collective-permute-start | bytes 786440 | tf_op jit(solution)/shard_map/ppermute | solution.py:438
  164.9 2.9 %collective-permute-start.24 = (f32[64,2048]{1,0:T(8,128)S(1)}, f32[64,2048]{1,0:T(8,128)S(1)}, u32[]{:S(2)}, u32[]{:S(2)}) collective-permute-start(f32[64,2048]{1,0:T(8,128)S(1)} %pad_maximum_fusion.4), channel_id=1, source_target_pairs={{0,4},{4,0},{8,12},{12,8},{16,20},{20,16},{24,28},{28,24},{1,5},{5... | collective-permute-start | bytes 1572872 | tf_op jit(solution)/shard_map/ppermute | solution.py:438
